TPU v7x, 32 devices: a whole 2x2x4 slice. The times are simulated.
32 devices in a mesh: vir: 8 (over z, y), fit: 4 (over x, core).
Axes of the slice: x: 2, y: 2, z: 4, core: 2. Of those that a mesh axis runs over, the one named last changes fastest.
Arguments:
- fitted: bfloat16 [2, 2400, 24, 7168], P(None, 'vir', None, 'fit'), may hold values from -0.0234375 to 0.0234375
- vcouple: bfloat16 [2, 2400, 2400], P(None, 'fit'), may hold values from -0.125 to 0.125
- actfock: float32 [2, 24, 24], replicated, may hold values from -1.25 to 1.25
- eps_vir: float32 [2400], P('vir'), may hold values from 0.5 to 4
- eps_act: float32 [24], replicated, may hold values from -0.5 to 0.5
- pair_energy: float32 [64], replicated, may hold values from -3 to -2
- source: float32 [2, 2400, 1536], P(None, 'vir'), may hold values from -6 to 6
Outputs:
- amplitude: float32 [2, 2400, 1536], P(None, 'vir')
All inputs are finite; a program needn't handle non-finite values.
Results may differ from a plain program's by a relative error of at most 0.0026.
Values may be sent and summed in bfloat16 or wider, within the bound.
A program may use at most 256 MiB of HBM per device.

v0:
```python
import jax
import jax.numpy as jnp
from jax import lax
from jax.sharding import PartitionSpec as P

PASSES = 3


def contract_first(left, right):
    return lax.dot_general(
        left, right, (((0,), (0,)), ((), ())), preferred_element_type=jnp.float32
    )


def plain_product(left, right):
    return jnp.dot(left, right, preferred_element_type=jnp.float32)


def active_coupling(values, actfock, active, pairs):
    highest = lax.Precision.HIGHEST
    local_vir = values.shape[1]
    grid = values.reshape(2, local_vir, active, pairs)
    act_real = jnp.einsum("aup,ut->atp", grid[0], actfock[0], precision=highest) - jnp.einsum(
        "aup,ut->atp", grid[1], actfock[1], precision=highest
    )
    act_imag = jnp.einsum("aup,ut->atp", grid[0], actfock[1], precision=highest) + jnp.einsum(
        "aup,ut->atp", grid[1], actfock[0], precision=highest
    )
    return jnp.stack([act_real, act_imag]).reshape(2, local_vir, actfock.shape[2] * pairs)


def per_device(fitted, vcouple, actfock, eps_vir, eps_act, pair_energy, source):
    local_vir = fitted.shape[1]
    active = fitted.shape[2]
    local_fit = fitted.shape[3]
    pairs = pair_energy.shape[0]
    block_rows = vcouple.shape[1]
    width = local_vir * active
    fit_index = lax.axis_index("fit")
    denominator = (
        eps_vir[:, None, None] + eps_act[None, :, None] - pair_energy[None, None, :]
    ).reshape(local_vir, active * pairs)
    amplitude = source / denominator[None]
    fit_real = fitted[0].reshape(width, local_fit)
    fit_imag = fitted[1].reshape(width, local_fit)
    for pass_index in range(PASSES):
        rounded = amplitude.astype(jnp.bfloat16)
        flat_both = jnp.concatenate(
            [rounded[0].reshape(width, pairs), rounded[1].reshape(width, pairs)], axis=1
        )
        real_side = contract_first(fit_real, flat_both)
        imag_side = contract_first(fit_imag, flat_both)
        over_real = real_side[:, :pairs] + imag_side[:, pairs:]
        over_imag = real_side[:, pairs:] - imag_side[:, :pairs]
        intersection = lax.psum(jnp.concatenate([over_real, over_imag], axis=1), "vir").astype(
            jnp.bfloat16
        )
        real_out = plain_product(fit_real, intersection)
        imag_out = plain_product(fit_imag, intersection)
        sum_real = real_out[:, :pairs] - imag_out[:, pairs:]
        sum_imag = real_out[:, pairs:] + imag_out[:, :pairs]
        fitted_part = jnp.stack([sum_real, sum_imag]).reshape(2, local_vir, active * pairs)
        regrouped = lax.all_to_all(rounded, "vir", split_axis=2, concat_axis=1, tiled=True)
        window = lax.dynamic_slice_in_dim(regrouped, fit_index * block_rows, block_rows, 1)
        couple_real = contract_first(vcouple[0], window[0]) - contract_first(vcouple[1], window[1])
        couple_imag = contract_first(vcouple[1], window[0]) + contract_first(vcouple[0], window[1])
        coupled = jnp.stack([couple_real, couple_imag])
        returned = lax.all_to_all(coupled, "vir", split_axis=1, concat_axis=2, tiled=True)
        fitted_part = fitted_part + returned
        total = lax.psum(fitted_part, "fit")
        part_amplitude = amplitude
        active_term = active_coupling(amplitude, actfock, active, pairs)
        residual = source - denominator[None] * part_amplitude - active_term - total
        updated = part_amplitude + residual / denominator[None]
        amplitude = updated
    return amplitude


def solution(mesh):
    return jax.shard_map(
        per_device,
        mesh=mesh,
        in_specs=(
            P(None, "vir", None, "fit"),
            P(None, "fit", None),
            P(),
            P("vir"),
            P(),
            P(),
            P(None, "vir", None),
        ),
        out_specs=P(None, "vir", None),
        check_vma=False,
    )
```

profile of v0, /device:TPU:0, one launch (start us, length us, event | category | flops | bytes accessed | tf_op | source)
XLA Modules:
  0.0 1272.0 jit_solution(17496041383994154291)
XLA Ops:
  6.5 7.8 copy.68
  14.7 6.0 broadcast_divide_fusion
  20.7 12.6 copy.82
  33.3 7.6 all-to-all-start
  40.9 34.1 %fusion.134 = (bf16[1,300,24,1792]{3,2,1,0:T(8,128)(2,1)}, bf16[1,300,24,1792]{3,2,1,0:T(8,128)(2,1)}) fusion(bf16[2,300,24,1792]{3,2,1,0:T(8,128)(2,1)} %param.7), kind=kLoop, calls=%fused_computation.183 | loop fusion | bytes 103219200 | tf_op jit(solution)/shard_map/slice | solution.py:44
  85.3 13.8 %convolution_bitcast_fusion.10 = f32[1792,128]{0,1:T(8,128)} fusion(bf16[7200,1792]{1,0:T(8,128)(2,1)} %bitcast.235, bf16[7200,64]{1,0:T(8,128)(2,1)S(1)} %reshape_squeeze.25, bf16[7200,64]{1,0:T(8,128)(2,1)} %reshape_squeeze.24), kind=kOutput, calls=%fused_computation.64 | convolution fusion | flops 3306700800 | bytes 28565504 | tf_op jit(solution)/shard_map/dot_general | solution.py:10
  103.6 5.1 all_to_all.81
  120.8 8.2 copy.85
  129.0 6.0 all-to-all-start.1
  135.0 12.6 convolution_bitcast_fusion.11
  147.8 131.9 %all-reduce.12 = bf16[1792,128]{0,1:T(8,128)(2,1)S(1)} all-reduce(f32[1792,128]{0,1:T(8,128)S(1)} %pad_maximum_fusion.6), channel_id=1, replica_groups=mesh['vir'=8,'fit'=4] {'vir'}, use_global_device_ids=true, to_apply=%region_0.0 | all-reduce | flops 229376 | bytes 1376256 | tf_op jit(solution)/shard_map/psum | solution.py:55
  279.7 11.9 convolution_bitcast_fusion.4
  291.6 11.9 convolution_bitcast_fusion.5
  303.6 5.0 slice_subtract_fusion.2
  322.0 7.8 copy.132
  329.8 5.7 maximum_add_fusion
  356.3 71.9 %all-reduce.7.cloned.1.call-done = f32[2,300,1536]{1,2,0:T(8,128)} async-done(((f32[2,300,1536]{1,2,0:T(8,128)}), f32[2,300,1536]{1,2,0:T(8,128)}) %all-reduce.7.cloned.1.call-update) | async-done | bytes 3686416 | tf_op jit(solution)/shard_map/psum | solution.py:70
  428.2 8.0 fusion.132
  437.5 12.6 copy.99
  450.1 6.1 all-to-all-start.2
  466.5 13.7 %convolution_bitcast_fusion.8 = f32[1792,128]{0,1:T(8,128)} fusion(bf16[7200,1792]{1,0:T(8,128)(2,1)} %bitcast.237, bf16[7200,64]{1,0:T(8,128)(2,1)S(1)} %reshape_squeeze.29, bf16[7200,64]{1,0:T(8,128)(2,1)} %reshape_squeeze.28), kind=kOutput, calls=%fused_computation.62 | convolution fusion | flops 3306700800 | bytes 28565504 | tf_op jit(solution)/shard_map/dot_general | solution.py:10
  480.3 29.6 %all-to-all-done.2 = bf16[2,300,1536]{1,0,2:T(2,128)(2,1)} async-done(((bf16[2,300,1536]{1,0,2:T(2,128)(2,1)}), bf16[2,300,1536]{1,0,2:T(2,128)(2,1)}, u32[]{:S(2)}, u32[]{:S(2)}) %all-to-all-start.2) | async-done | bytes 1843232 | tf_op jit(solution)/shard_map/all_to_all | solution.py:63
  531.3 8.4 copy.102
  544.3 12.6 convolution_bitcast_fusion.9
  557.1 130.6 %all-reduce.13 = bf16[1792,128]{0,1:T(8,128)(2,1)S(1)} all-reduce(f32[1792,128]{0,1:T(8,128)S(1)} %pad_maximum_fusion.7), channel_id=1, replica_groups=mesh['vir'=8,'fit'=4] {'vir'}, use_global_device_ids=true, to_apply=%region_2.0 | all-reduce | flops 229376 | bytes 1376256 | tf_op jit(solution)/shard_map/psum | solution.py:55
  687.7 11.9 convolution_bitcast_fusion.2
  699.7 11.9 convolution_bitcast_fusion.3
  711.6 5.0 slice_subtract_fusion.1
  730.0 7.9 copy.133
  737.9 5.7 maximum_add_fusion.1
  764.6 72.5 %all-reduce.9.cloned.1.call-done = f32[2,300,1536]{1,2,0:T(8,128)} async-done(((f32[2,300,1536]{1,2,0:T(8,128)}), f32[2,300,1536]{1,2,0:T(8,128)}) %all-reduce.9.cloned.1.call-update) | async-done | bytes 3686416 | tf_op jit(solution)/shard_map/psum | solution.py:70
  837.2 9.3 fusion.130
  847.9 12.6 copy.116
  860.5 5.9 all-to-all-start.4
  876.7 13.8 %convolution_bitcast_fusion.6 = f32[1792,128]{0,1:T(8,128)} fusion(bf16[7200,1792]{1,0:T(8,128)(2,1)} %bitcast.239, bf16[7200,64]{1,0:T(8,128)(2,1)S(1)} %reshape_squeeze.31, bf16[7200,64]{1,0:T(8,128)(2,1)} %reshape_squeeze.30), kind=kOutput, calls=%fused_computation.60 | convolution fusion | flops 3306700800 | bytes 28565504 | tf_op jit(solution)/shard_map/dot_general | solution.py:10
  890.5 29.5 %all-to-all-done.4 = bf16[2,300,1536]{1,0,2:T(2,128)(2,1)} async-done(((bf16[2,300,1536]{1,0,2:T(2,128)(2,1)}), bf16[2,300,1536]{1,0,2:T(2,128)(2,1)}, u32[]{:S(2)}, u32[]{:S(2)}) %all-to-all-start.4) | async-done | bytes 1843232 | tf_op jit(solution)/shard_map/all_to_all | solution.py:63
  924.4 4.9 all_to_all.97
  941.4 8.6 copy.119
  954.7 12.6 convolution_bitcast_fusion.7
  967.5 130.5 %all-reduce.14 = bf16[1792,128]{0,1:T(8,128)(2,1)S(1)} all-reduce(f32[1792,128]{0,1:T(8,128)S(1)} %pad_maximum_fusion.8), channel_id=1, replica_groups=mesh['vir'=8,'fit'=4] {'vir'}, use_global_device_ids=true, to_apply=%region_4.0 | all-reduce | flops 229376 | bytes 1376256 | tf_op jit(solution)/shard_map/psum | solution.py:55
  1098.0 11.9 convolution_bitcast_fusion
  1109.9 11.9 convolution_bitcast_fusion.1
  1121.9 5.1 slice_subtract_fusion
  1140.4 7.8 copy.134
  1148.3 5.6 maximum_add_fusion.2
  1174.7 73.3 %all-reduce.11.cloned.1.call-done = f32[2,300,1536]{1,2,0:T(8,128)} async-done(((f32[2,300,1536]{1,2,0:T(8,128)}), f32[2,300,1536]{1,2,0:T(8,128)}) %all-reduce.11.cloned.1.call-update) | async-done | bytes 3686416 | tf_op jit(solution)/shard_map/psum | solution.py:70
  1248.0 9.3 fusion.8
  1257.3 8.0 copy.122
  (144 shorter events, 201.0 us)
Async XLA Ops:
  6.5 7.8 copy-start.19
  6.5 7.8 copy-start.18
  6.5 7.8 copy-start.17
  14.7 6.0 copy-start
  33.3 65.8 %all-to-all-start = ((bf16[2,300,1536]{1,0,2:T(2,128)(2,1)}), bf16[2,300,1536]{1,0,2:T(2,128)(2,1)}, u32[]{:S(2)}, u32[]{:S(2)}) async-start(bf16[2,300,1536]{1,0,2:T(2,128)(2,1)} %copy.82), calls=%async_computation | async-start | bytes 4718592 | tf_op jit(solution)/shard_map/all_to_all | solution.py:63
  76.3 4.1 copy-start.8
  103.6 11.1 slice-start
  108.7 6.0 slice-start.1
  129.0 193.0 %all-to-all-start.1 = ((f32[2,2400,192]{2,0,1:T(2,128)}), f32[2,2400,192]{2,0,1:T(2,128)}, u32[]{:S(2)}, u32[]{:S(2)}) async-start(f32[2,2400,192]{2,0,1:T(2,128)} %copy.85), calls=%async_computation.1 | async-start | bytes 9830400 | tf_op jit(solution)/shard_map/all_to_all | solution.py:68
  135.0 293.2 %all-reduce.7.cloned.1.call-start = ((), (), s32[]{:S(2)}) async-start(), calls=%async_computation.6 | async-start | bytes 9437184 | tf_op jit(solution)/shard_map/psum | solution.py:70
  135.0 12.6 copy-start.12
  335.5 2.7 copy-start.14
  354.4 73.7 %copy-start.1 = (f32[300,1536]{0,1:T(8,128)S(1)}, f32[300,1536]{0,1:T(8,128)}, u32[]{:S(2)}) copy-start(f32[300,1536]{0,1:T(8,128)} %copy-done) | copy-start | bytes 5529604
  436.1 1.4 copy-start.6
  450.1 6.1 copy-start.7
  450.1 59.7 %all-to-all-start.2 = ((bf16[2,300,1536]{1,0,2:T(2,128)(2,1)}), bf16[2,300,1536]{1,0,2:T(2,128)(2,1)}, u32[]{:S(2)}, u32[]{:S(2)}) async-start(bf16[2,300,1536]{1,0,2:T(2,128)(2,1)} %copy.99), calls=%async_computation.2 | async-start | bytes 4718592 | tf_op jit(solution)/shard_map/all_to_all | solution.py:63
  457.5 4.0 copy-start.9
  509.8 15.3 %slice-start.2 = ((s8[5836800]{0:T(1024)(128)(4,1)}), s8[1642496]{0:T(1024)(128)(4,1)S(1)}, s32[]{:S(2)}) async-start(s8[5836800]{0:T(1024)(128)(4,1)} %bitcast.243), calls=%async_computation.11 | async-start | bytes 3284992
  519.1 6.0 slice-start.3
  539.6 190.4 %all-to-all-start.3 = ((f32[2,2400,192]{2,0,1:T(2,128)}), f32[2,2400,192]{2,0,1:T(2,128)}, u32[]{:S(2)}, u32[]{:S(2)}) async-start(f32[2,2400,192]{2,0,1:T(2,128)} %copy.102), calls=%async_computation.3 | async-start | bytes 9830400 | tf_op jit(solution)/shard_map/all_to_all | solution.py:68
  544.3 12.6 copy-start.13
  544.3 292.9 %all-reduce.9.cloned.1.call-start = ((), (), s32[]{:S(2)}) async-start(), calls=%async_computation.7 | async-start | bytes 9437184 | tf_op jit(solution)/shard_map/psum | solution.py:70
  743.7 2.7 copy-start.15
  762.8 74.4 %copy-start.2 = (f32[300,1536]{0,1:T(8,128)S(1)}, f32[300,1536]{0,1:T(8,128)}, u32[]{:S(2)}) copy-start(f32[300,1536]{0,1:T(8,128)} %copy-done) | copy-start | bytes 5529604
  846.5 1.4 copy-start.4
  860.5 5.9 copy-start.5
  860.5 59.4 %all-to-all-start.4 = ((bf16[2,300,1536]{1,0,2:T(2,128)(2,1)}), bf16[2,300,1536]{1,0,2:T(2,128)(2,1)}, u32[]{:S(2)}, u32[]{:S(2)}) async-start(bf16[2,300,1536]{1,0,2:T(2,128)(2,1)} %copy.116), calls=%async_computation.4 | async-start | bytes 4718592 | tf_op jit(solution)/shard_map/all_to_all | solution.py:63
  867.7 4.0 copy-start.10
  924.4 10.9 slice-start.4
  929.3 6.0 slice-start.5
  950.0 190.4 %all-to-all-start.5 = ((f32[2,2400,192]{2,0,1:T(2,128)}), f32[2,2400,192]{2,0,1:T(2,128)}, u32[]{:S(2)}, u32[]{:S(2)}) async-start(f32[2,2400,192]{2,0,1:T(2,128)} %copy.119), calls=%async_computation.5 | async-start | bytes 9830400 | tf_op jit(solution)/shard_map/all_to_all | solution.py:68
  954.6 12.6 copy-start.11
  954.6 293.4 %all-reduce.11.cloned.1.call-start = ((), (), s32[]{:S(2)}) async-start(), calls=%async_computation.8 | async-start | bytes 9437184 | tf_op jit(solution)/shard_map/psum | solution.py:70
  1153.9 2.7 copy-start.16
  1172.8 75.2 %copy-start.3 = (f32[300,1536]{0,1:T(8,128)S(1)}, f32[300,1536]{0,1:T(8,128)}, u32[]{:S(2)}) copy-start(f32[300,1536]{0,1:T(8,128)} %copy-done) | copy-start | bytes 5529604
Sparse Core Ops, SparseCore 0:
  335.6 92.4 all-reduce.6
  743.8 93.3 all-reduce.8
  1154.1 93.9 all-reduce.10
where the time goes:
time: 1280 us; the launch traced here: 1270 us
  blocking collectives  393 us (31%)
  waiting for transfers between devices  277 us (22%)
  local copies, waits for them, and re-layouts  258 us (20%)
  matrix products  224 us (18%)
  other arithmetic  71.9 us (6%)
  starting transfers between devices  34.9 us (3%)
  between operations  14.1 us (1%)
    psum x3, blocking collectives, per_device(): lax.psum(jnp.concatenate([over_real, over_imag], axis=1), 'vir')  393 us
    psum x3, waiting for transfers between devices, per_device(): total = lax.psum(fitted_part, 'fit')  218 us
    dot_general x18, matrix products, contract_first(): lax.dot_general(left, right, (((0,), (0,)), ((), ())), preferred_element_...  109 us
    dot_general x6, matrix products, plain_product(): return jnp.dot(left, right, preferred_element_type=jnp.float32)  71.5 us
    all_to_all x3, waiting for transfers between devices, per_device(): lax.all_to_all(rounded, 'vir', split_axis=2, concat_axis=1, tiled=True)  59.1 us
    another operation x12, local copies, waits for them, and re-layouts, per_device(): jnp.stack([sum_real, sum_imag]).reshape(2, local_vir, active * pairs)  40.3 us
    convert_element_type x3, local copies, waits for them, and re-layouts, per_device(): rounded = amplitude.astype(jnp.bfloat16)  37.8 us
    slice x1, local copies, waits for them, and re-layouts, per_device(): fit_real = fitted[0].reshape(width, local_fit)  34.1 us
  transfers between devices with their start and end apart: 9, of which 5 were waited for; matrix products, arithmetic and copies ran while one was open for 26% of the time, Pallas kernels for 0%

commit v1 on v0

--- a/solution.py
+++ b/solution.py
@@ -1,6 +1,8 @@
 import jax
 import jax.numpy as jnp
 from jax import lax
+from jax.experimental import pallas as pl
+from jax.experimental.pallas import tpu as pltpu
 from jax.sharding import PartitionSpec as P
 
 PASSES = 3
@@ -29,7 +31,7 @@
     return jnp.stack([act_real, act_imag]).reshape(2, local_vir, actfock.shape[2] * pairs)
 
 
-def per_device(fitted, vcouple, actfock, eps_vir, eps_act, pair_energy, source):
+def plain_device(fitted, vcouple, actfock, eps_vir, eps_act, pair_energy, source):
     local_vir = fitted.shape[1]
     active = fitted.shape[2]
     local_fit = fitted.shape[3]
@@ -76,9 +78,233 @@
     return amplitude
 
 
+ROW_CHUNKS = 3
+ROW_TILE = 512
+VIR_TILE = 16
+
+
+def turn(values, pairs):
+    return jnp.concatenate([-values[..., pairs:], values[..., :pairs]], axis=-1)
+
+
+def swap(values, bit):
+    size = lax.axis_size("fit")
+    return lax.ppermute(values, "fit", [(i, i ^ bit) for i in range(size)])
+
+
+def pick(values, index, axis):
+    return lax.dynamic_index_in_dim(values, index, axis, keepdims=False)
+
+
+def fit_reduce(values, index):
+    size = lax.axis_size("fit")
+    stage = 1
+    values = values.reshape(size, -1, values.shape[-1])
+    while stage < size:
+        left = values.shape[0]
+        grid = values.reshape(left // 2, 2, *values.shape[1:])
+        side = (index // stage) % 2
+        sent = pick(grid, 1 - side, 1).astype(jnp.bfloat16)
+        values = pick(grid, side, 1) + swap(sent, stage).astype(jnp.float32)
+        stage *= 2
+    return values[0]
+
+
+def fit_gather(values, index):
+    size = lax.axis_size("fit")
+    stage = size // 2
+    values = values[None]
+    while stage >= 1:
+        other = swap(values, stage)
+        side = (index // stage) % 2
+        first = jnp.where(side == 0, values, other)
+        second = jnp.where(side == 0, other, values)
+        values = jnp.stack([first, second], axis=1).reshape(-1, *values.shape[1:])
+        stage //= 2
+    return values.reshape(-1, values.shape[-1])
+
+
+def vir_sum(values):
+    size = lax.axis_size("vir")
+    rows, lanes = values.shape
+    parts = lax.all_to_all(
+        values.astype(jnp.bfloat16).reshape(size, rows // size, lanes), "vir", 0, 0
+    )
+    own = jnp.sum(parts.astype(jnp.float32), axis=0).astype(jnp.bfloat16)
+    spread = jnp.broadcast_to(own[None], (size, rows // size, lanes))
+    return lax.all_to_all(spread, "vir", 0, 0).reshape(rows, lanes)
+
+
+def back_kernel(fit_ref, inter_ref, turned_ref, virtual_ref, out_ref):
+    out_ref[...] = (
+        plain_product(fit_ref[0], inter_ref[...])
+        + plain_product(fit_ref[1], turned_ref[...])
+        + virtual_ref[...]
+    )
+
+
+def tile_of(rows):
+    return max(t for t in range(16, ROW_TILE + 1, 16) if rows % t == 0)
+
+
+def back_product(fit_rows, inter, turned, virtual, first, rows):
+    depth, lanes = inter.shape
+    tile = tile_of(rows)
+    skip = first // tile
+    return pl.pallas_call(
+        back_kernel,
+        grid=(rows // tile,),
+        in_specs=[
+            pl.BlockSpec((2, tile, depth), lambda i: (0, i + skip, 0)),
+            pl.BlockSpec((depth, lanes), lambda i: (0, 0)),
+            pl.BlockSpec((depth, lanes), lambda i: (0, 0)),
+            pl.BlockSpec((tile, lanes), lambda i: (i + skip, 0)),
+        ],
+        out_specs=pl.BlockSpec((tile, lanes), lambda i: (i, 0)),
+        out_shape=jax.ShapeDtypeStruct((rows, lanes), jnp.float32),
+        cost_estimate=pl.CostEstimate(
+            flops=4 * rows * depth * lanes,
+            bytes_accessed=4 * rows * depth + 8 * rows * lanes,
+            transcendentals=0,
+        ),
+        compiler_params=pltpu.CompilerParams(vmem_limit_bytes=24 * 2**20),
+    )(fit_rows, inter, turned, virtual)
+
+
+def virtual_kernel(pairs, couple_ref, rows_ref, out_ref):
+    lanes = 2 * pairs
+    for t in range(out_ref.shape[1]):
+        block = rows_ref[:, t * lanes : (t + 1) * lanes]
+        out_ref[:, t, :] = plain_product(couple_ref[0], block) + plain_product(
+            couple_ref[1], turn(block, pairs)
+        )
+
+
+def virtual_product(couple, rows, active, pairs):
+    lanes = 2 * pairs
+    out, depth = couple.shape[1:]
+    group = 8
+    return pl.pallas_call(
+        lambda *refs: virtual_kernel(pairs, *refs),
+        grid=(active // group,),
+        in_specs=[
+            pl.BlockSpec((2, out, depth), lambda i: (0, 0, 0)),
+            pl.BlockSpec((depth, group * lanes), lambda i: (0, i)),
+        ],
+        out_specs=pl.BlockSpec((out, group, lanes), lambda i: (0, i, 0)),
+        out_shape=jax.ShapeDtypeStruct((out, active, lanes), jnp.float32),
+        cost_estimate=pl.CostEstimate(
+            flops=4 * out * depth * active * lanes,
+            bytes_accessed=2 * depth * active * lanes + 4 * out * active * lanes,
+            transcendentals=0,
+        ),
+        compiler_params=pltpu.CompilerParams(vmem_limit_bytes=24 * 2**20),
+    )(couple, rows)
+
+
+def per_device(fitted, vcouple, actfock, eps_vir, eps_act, pair_energy, source):
+    n_fit, n_vir = lax.axis_size("fit"), lax.axis_size("vir")
+    fit_index, vir_index = lax.axis_index("fit"), lax.axis_index("vir")
+    local_vir, active, local_fit = fitted.shape[1:]
+    pairs = pair_energy.shape[0]
+    lanes = 2 * pairs
+    spread = n_vir // n_fit
+    chunk_vir = local_vir // ROW_CHUNKS
+    own_vir = chunk_vir // n_fit
+    chunk_rows = chunk_vir * active
+    highest = lax.Precision.HIGHEST
+
+    denominator = eps_vir[:, None, None] + eps_act[None, :, None] - pair_energy[None, None, :]
+    denominator = jnp.concatenate([denominator, denominator], axis=2)
+    grid = source.reshape(2, local_vir, active, pairs)
+    joined = jnp.concatenate([grid[0], grid[1]], axis=2)
+    start = joined / denominator
+
+    def own(values, chunk):
+        return lax.dynamic_slice_in_dim(
+            values, chunk * chunk_vir + fit_index * own_vir, own_vir, 0
+        )
+
+    own_source = [own(joined, c) for c in range(ROW_CHUNKS)]
+    own_denominator = [own(denominator, c) for c in range(ROW_CHUNKS)]
+    own_start = [own(start, c) for c in range(ROW_CHUNKS)]
+    amplitude = own_start
+    fit_rows = fitted.reshape(2, local_vir * active, local_fit)
+    own_rows = ROW_CHUNKS * own_vir
+    padded = -(-own_rows // VIR_TILE) * VIR_TILE
+    couple = lax.dynamic_slice_in_dim(vcouple, vir_index * local_vir, local_vir, 2)
+    couple = couple.reshape(2, spread, ROW_CHUNKS, n_fit, own_vir, local_vir)
+    couple = couple.transpose(0, 5, 1, 3, 2, 4).reshape(2, local_vir, n_vir, own_rows)
+    couple = jnp.pad(couple, ((0, 0), (0, 0), (0, 0), (0, padded - own_rows)))
+    couple = couple.reshape(2, local_vir, n_vir * padded)
+    gathered = [
+        start[c * chunk_vir : (c + 1) * chunk_vir].reshape(chunk_rows, lanes).astype(jnp.bfloat16)
+        for c in range(ROW_CHUNKS)
+    ]
+    own_rounded = [a.astype(jnp.bfloat16) for a in amplitude]
+    route = [
+        (u * n_fit + g, ((u % spread) * n_fit + g) * n_fit + u // spread)
+        for u in range(n_vir)
+        for g in range(n_fit)
+    ]
+    fit_whole = fitted.reshape(2 * local_vir * active, local_fit)
+    for pass_index in range(PASSES):
+        mine = jnp.concatenate(own_rounded).reshape(own_rows, active * lanes)
+        mine = jnp.pad(mine, ((0, padded - own_rows), (0, 0)))
+        moved = lax.ppermute(mine, ("vir", "fit"), route)
+        rows = lax.all_gather(moved, "vir", axis=0, tiled=True)
+        virtual = virtual_product(couple, rows, active, pairs)
+        virtual = virtual.reshape(local_vir * active, lanes)
+
+        both = jnp.concatenate(gathered + [-turn(g, pairs) for g in gathered])
+        inter = vir_sum(contract_first(fit_whole, both))
+        inter_turned = turn(inter, pairs)
+        last = pass_index == PASSES - 1
+        updated = []
+        gathered = []
+        for c in range(ROW_CHUNKS):
+            term = back_product(
+                fit_rows, inter, inter_turned, virtual, c * chunk_rows, chunk_rows
+            )
+            total = fit_reduce(term, fit_index).reshape(own_vir, active, lanes)
+            value = amplitude[c]
+            act = jnp.einsum("aul,ut->atl", value, actfock[0], precision=highest) + jnp.einsum(
+                "aul,ut->atl", turn(value, pairs), actfock[1], precision=highest
+            )
+            residual = own_source[c] - own_denominator[c] * value - act - total
+            value = value + residual / own_denominator[c]
+            updated.append(value)
+            sent = value - own_start[c] if last else value
+            gathered.append(
+                fit_gather(sent.reshape(-1, lanes).astype(jnp.bfloat16), fit_index)
+            )
+        amplitude = updated
+        own_rounded = [a.astype(jnp.bfloat16) for a in amplitude]
+    change = jnp.concatenate(gathered).reshape(local_vir, active, lanes).astype(jnp.float32)
+    result = start + change
+    return jnp.stack([result[..., :pairs], result[..., pairs:]]).reshape(source.shape)
+
+
+def choose(mesh):
+    def body(*args):
+        n_fit, n_vir = mesh.shape["fit"], mesh.shape["vir"]
+        fitted = args[0]
+        fits = (
+            n_vir % n_fit == 0
+            and n_fit & (n_fit - 1) == 0
+            and fitted.shape[1] % (ROW_CHUNKS * n_fit) == 0
+            and fitted.shape[2] % 8 == 0
+            and fitted.shape[3] % (16 * n_vir) == 0
+            and fitted.shape[1] * fitted.shape[2] % (16 * ROW_CHUNKS) == 0
+        )
+        return per_device(*args) if fits else plain_device(*args)
+
+    return body
+
+
 def solution(mesh):
     return jax.shard_map(
-        per_device,
+        choose(mesh),
         mesh=mesh,
         in_specs=(
             P(None, "vir", None, "fit"),

time: 1280 us -> 621 us (0.49)
  blocking collectives: 393 us -> 0 us
  local copies, waits for them, and re-layouts: 258 us -> 73.8 us
  matrix products: 224 us -> 87.3 us
  Pallas kernels: 0 us -> 108 us
  waiting for transfers between devices: 277 us -> 181 us
  starting transfers between devices: 34.9 us -> 99.2 us
  other arithmetic: 71.9 us -> 47.8 us
    psum x3 -> x0, blocking collectives: 393 us -> none  [per_device(): lax.psum(jnp.concatenate([over_real, over_imag], axis=1), 'vir')]
    psum x3 -> x0, waiting for transfers between devices: 218 us -> none  [per_device(): total = lax.psum(fitted_part, 'fit')]
    pallas_call x0 -> x12, Pallas kernels: none -> 108 us  [the longest x9 83.4 us: back_product(): pl.pallas_call(back_kernel, grid=(rows // tile,), in_specs=[pl.BlockSpec(...]
    dot_general x18, matrix products: 115 us -> 27.5 us  [the longest x9 14.7 us: per_device(): jnp.einsum('aul,ut->atl', turn(value, pairs), actfock[1], precision=highest)]
    ppermute x0 -> x39, waiting for transfers between devices: none -> 80.3 us  [the longest x36 80.3 us: swap(): return lax.ppermute(values, 'fit', [(i, i ^ bit) for i in range(size)])]
    another operation x21 -> x9, local copies, waits for them, and re-layouts: 84.1 us -> 8.3 us  [the longest x1 7.97 us: per_device(): jnp.stack([result[..., :pairs], result[..., pairs:]]).reshape(source.shape)]
    all_to_all x9 -> x0, local copies, waits for them, and re-layouts: 51.7 us -> none  [the longest x6 28.1 us: per_device(): lax.all_to_all(rounded, 'vir', split_axis=2, concat_axis=1, tiled=True)]
    dot_general x18 -> x3, matrix products: 109 us -> 59.9 us  [contract_first(): lax.dot_general(left, right, (((0,), (0,)), ((), ())), preferred_element_...]
  transfers between devices with their start and end apart: 9 -> 48, of which waited for: 5 -> 26; matrix products, arithmetic and copies ran while one was open for 26% -> 23% of each run, Pallas kernels for 0% -> 5%
where the time goes in v1:
time: 621 us; the launch traced here: 613 us
  waiting for transfers between devices  181 us (29%)
  Pallas kernels  108 us (17%)
  starting transfers between devices  99.2 us (16%)
  matrix products  87.3 us (14%)
  local copies, waits for them, and re-layouts  73.8 us (12%)
  other arithmetic  47.8 us (8%)
  between operations  15.1 us (2%)
    pallas_call x9, Pallas kernels, back_product(): pl.pallas_call(back_kernel, grid=(rows // tile,), in_specs=[pl.BlockSpec(...  83.4 us
    ppermute x36, waiting for transfers between devices, swap(): return lax.ppermute(values, 'fit', [(i, i ^ bit) for i in range(size)])  80.3 us
    dot_general x3, matrix products, contract_first(): lax.dot_general(left, right, (((0,), (0,)), ((), ())), preferred_element_...  59.9 us
    all_to_all x3, waiting for transfers between devices, vir_sum(): return lax.all_to_all(spread, 'vir', 0, 0).reshape(rows, lanes)  47.8 us
    all_to_all x3, waiting for transfers between devices, vir_sum(): lax.all_to_all(values.astype(jnp.bfloat16).reshape(size, rows // size, la...  46.5 us
    all_to_all x3, starting transfers between devices, vir_sum(): lax.all_to_all(values.astype(jnp.bfloat16).reshape(size, rows // size, la...  42.4 us
    ppermute x36, starting transfers between devices, swap(): return lax.ppermute(values, 'fit', [(i, i ^ bit) for i in range(size)])  29.6 us
    unnamed x110, local copies, waits for them, and re-layouts  25.4 us
  transfers between devices with their start and end apart: 48, of which 26 were waited for; matrix products, arithmetic and copies ran while one was open for 23% of the time, Pallas kernels for 5%

profile of v1, /device:TPU:0, one launch (start us, length us, event | category | flops | bytes accessed | tf_op | source)
XLA Modules:
  0.0 612.6 jit_solution(15194284762989623805)
XLA Ops:
  6.5 8.2 %fusion.149 = (f32[1,300,1536]{2,0,1:T(1,128)}, f32[1,300,1536]{2,0,1:T(1,128)}) fusion(f32[2,300,1536]{2,0,1:T(2,128)} %param.13), kind=kLoop, calls=%fused_computation.318 | loop fusion | bytes 7372800 | tf_op jit(solution)/shard_map/slice | solution.py:220
  14.7 3.6 copy.40
  18.3 3.5 copy.15
  21.8 3.6 copy.39
  25.5 3.3 copy.14
  31.7 7.2 %fusion.147 = (bf16[300,24,128]{2,1,0:T(8,128)(2,1)S(1)}, f32[300,24,128]{2,1,0:T(8,128)S(1)}) fusion(f32[300,24,64]{2,1,0:T(8,128)} %broadcast_subtract_fusion, f32[300,24,64]{2,1,0:T(8,128)} %copy.15, f32[300,24,64]{2,1,0:T(8,128)} %copy.14), kind=kLoop, calls=%fused_computation.316 | loop fusion | flops 3686400 | bytes 11059200 | tf_op jit(solution)/shard_map/convert.6
  48.7 19.5 %fusion = bf16[1792,128]{0,1:T(8,128)(2,1)S(1)} fusion(bf16[14400,128]{1,0:T(8,128)(2,1)} %fusion.23, bf16[14400,1792]{1,0:T(8,128)(2,1)} %bitcast.430), kind=kOutput, calls=%fused_computation.18 | convolution fusion | flops 6606258176 | bytes 55754752 | tf_op jit(solution)/shard_map/dot_general | solution.py:12
  69.2 33.3 %all-to-all-start = ((bf16[8,224,128]{2,1,0:T(8,128)(2,1)}), bf16[8,224,128]{2,1,0:T(8,128)(2,1)S(1)}, u32[]{:S(2)}, u32[]{:S(2)}) async-start(bf16[8,224,128]{2,1,0:T(8,128)(2,1)} %bitcast.13), calls=%async_computation | async-start | bytes 917504 | tf_op jit(solution)/shard_map/all_to_all | solution.py:130
  112.3 5.8 all-to-all-done
  119.0 8.3 %all-to-all-start.1 = ((bf16[8,224,128]{2,1,0:T(8,128)(2,1)}), bf16[8,224,128]{2,1,0:T(8,128)(2,1)S(1)}, u32[]{:S(2)}, u32[]{:S(2)}) async-start(bf16[8,224,128]{2,1,0:T(8,128)(2,1)} %broadcast_in_dim.6), calls=%async_computation.1 | async-start | bytes 917504 | tf_op jit(solution)/shard_map/all_to_all | solution.py:135
  142.2 12.0 %all-to-all-done.1 = bf16[8,224,128]{2,1,0:T(8,128)(2,1)S(1)} async-done(((bf16[8,224,128]{2,1,0:T(8,128)(2,1)}), bf16[8,224,128]{2,1,0:T(8,128)(2,1)S(1)}, u32[]{:S(2)}, u32[]{:S(2)}) %all-to-all-start.1) | async-done | bytes 458784 | tf_op jit(solution)/shard_map/all_to_all | solution.py:135
  154.6 4.6 all-gather.4.cloned.1.call-done.refs_1_
  161.3 8.4 %shard_map.73 = f32[300,24,128]{2,1,0:T(8,128)S(1)} custom-call(bf16[2,300,640]{2,1,0:T(8,128)(2,1)S(1)} %copy.22.refs_0_, bf16[640,3072]{1,0:T(8,128)(2,1)S(1)} %copy-done), custom_call_target="tpu_custom_call" | custom-call | flops 2359296000 | bytes 7618560 | tf_op jit(solution)/shard_map/pallas_call | solution.py:187
  169.7 9.3 %shard_map.75 = f32[2400,128]{1,0:T(8,128)S(1)} custom-call(bf16[2,7200,1792]{2,1,0:T(8,128)(2,1)} %bitcast.431, bf16[1792,128]{1,0:T(8,128)(2,1)S(1)} %bitcast.401, bf16[1792,128]{1,0:T(8,128)(2,1)S(1)} %pad_maximum_fusion.14.turned_ref, f32[7200,128]{1,0:T(8,128)S(1)} %bitcast.394), custom_call_target="tpu_custom_call" | custom-call | flops 2202009600 | bytes 19660800 | tf_op jit(solution)/shard_map/pallas_call | solution.py:154
  178.9 9.3 %shard_map.74 = f32[2400,128]{1,0:T(8,128)S(1)} custom-call(bf16[2,7200,1792]{2,1,0:T(8,128)(2,1)} %bitcast.432, bf16[1792,128]{1,0:T(8,128)(2,1)S(1)} %bitcast.402, bf16[1792,128]{1,0:T(8,128)(2,1)S(1)} %pad_maximum_fusion.14.turned_ref, f32[7200,128]{1,0:T(8,128)S(1)} %bitcast.395), custom_call_target="tpu_custom_call" | custom-call | flops 2202009600 | bytes 19660800 | tf_op jit(solution)/shard_map/pallas_call | solution.py:154
  188.9 9.2 %shard_map.76 = f32[2400,128]{1,0:T(8,128)S(1)} custom-call(bf16[2,7200,1792]{2,1,0:T(8,128)(2,1)} %bitcast.433, bf16[1792,128]{1,0:T(8,128)(2,1)S(1)} %bitcast.403, bf16[1792,128]{1,0:T(8,128)(2,1)S(1)} %pad_maximum_fusion.14.turned_ref, f32[7200,128]{1,0:T(8,128)S(1)} %bitcast.396), custom_call_target="tpu_custom_call" | custom-call | flops 2202009600 | bytes 19660800 | tf_op jit(solution)/shard_map/pallas_call | solution.py:154
  198.5 3.1 collective-permute-start.6
  206.4 3.3 collective-permute-done.2
  209.7 3.1 collective-permute-done.10
  222.5 22.1 %collective-permute-done.7 = bf16[1,600,128]{2,1,0:T(8,128)(2,1)S(1)} collective-permute-done((bf16[1,600,128]{2,1,0:T(8,128)(2,1)S(1)}, bf16[1,600,128]{2,1,0:T(8,128)(2,1)S(1)}, u32[]{:S(2)}, u32[]{:S(2)}) %collective-permute-start.7) | collective-permute-done | bytes 153632 | tf_op jit(solution)/shard_map/ppermute | solution.py:92
  256.7 20.2 %fusion.1 = bf16[1792,128]{0,1:T(8,128)(2,1)S(1)} fusion(bf16[14400,128]{1,0:T(8,128)(2,1)} %fusion.26, bf16[14400,1792]{1,0:T(8,128)(2,1)} %bitcast.434), kind=kOutput, calls=%fused_computation.19 | convolution fusion | flops 6606258176 | bytes 55754752 | tf_op jit(solution)/shard_map/dot_general | solution.py:12
  277.9 4.6 all-to-all-start.2
  284.8 22.0 %all-to-all-done.2 = bf16[8,224,128]{2,1,0:T(8,128)(2,1)S(1)} async-done(((bf16[8,224,128]{2,1,0:T(8,128)(2,1)}), bf16[8,224,128]{2,1,0:T(8,128)(2,1)S(1)}, u32[]{:S(2)}, u32[]{:S(2)}) %all-to-all-start.2) | async-done | bytes 458784 | tf_op jit(solution)/shard_map/all_to_all | solution.py:130
  307.8 5.8 all-to-all-start.3
  317.8 18.9 %all-to-all-done.3 = bf16[8,224,128]{2,1,0:T(8,128)(2,1)S(1)} async-done(((bf16[8,224,128]{2,1,0:T(8,128)(2,1)}), bf16[8,224,128]{2,1,0:T(8,128)(2,1)S(1)}, u32[]{:S(2)}, u32[]{:S(2)}) %all-to-all-start.3) | async-done | bytes 458784 | tf_op jit(solution)/shard_map/all_to_all | solution.py:135
  340.3 8.4 %shard_map.77 = f32[300,24,128]{2,1,0:T(8,128)S(1)} custom-call(bf16[2,300,640]{2,1,0:T(8,128)(2,1)S(1)} %copy.22.refs_0_, bf16[640,3072]{1,0:T(8,128)(2,1)S(1)} %copy-done.2), custom_call_target="tpu_custom_call" | custom-call | flops 2359296000 | bytes 7618560 | tf_op jit(solution)/shard_map/pallas_call | solution.py:187
  348.7 9.2 %shard_map.78 = f32[2400,128]{1,0:T(8,128)S(1)} custom-call(bf16[2,7200,1792]{2,1,0:T(8,128)(2,1)} %bitcast.435, bf16[1792,128]{1,0:T(8,128)(2,1)S(1)} %bitcast.409, bf16[1792,128]{1,0:T(8,128)(2,1)S(1)} %pad_maximum_fusion.15.turned_ref, f32[7200,128]{1,0:T(8,128)S(1)} %bitcast.397), custom_call_target="tpu_custom_call" | custom-call | flops 2202009600 | bytes 19660800 | tf_op jit(solution)/shard_map/pallas_call | solution.py:154
  358.0 9.3 %shard_map.79 = f32[2400,128]{1,0:T(8,128)S(1)} custom-call(bf16[2,7200,1792]{2,1,0:T(8,128)(2,1)} %bitcast.436, bf16[1792,128]{1,0:T(8,128)(2,1)S(1)} %bitcast.410, bf16[1792,128]{1,0:T(8,128)(2,1)S(1)} %pad_maximum_fusion.15.turned_ref, f32[7200,128]{1,0:T(8,128)S(1)} %bitcast.398), custom_call_target="tpu_custom_call" | custom-call | flops 2202009600 | bytes 19660800 | tf_op jit(solution)/shard_map/pallas_call | solution.py:154
  368.0 9.4 %shard_map.80 = f32[2400,128]{1,0:T(8,128)S(1)} custom-call(bf16[2,7200,1792]{2,1,0:T(8,128)(2,1)} %bitcast.437, bf16[1792,128]{1,0:T(8,128)(2,1)S(1)} %bitcast.411, bf16[1792,128]{1,0:T(8,128)(2,1)S(1)} %pad_maximum_fusion.15.turned_ref, f32[7200,128]{1,0:T(8,128)S(1)} %bitcast.399), custom_call_target="tpu_custom_call" | custom-call | flops 2202009600 | bytes 19660800 | tf_op jit(solution)/shard_map/pallas_call | solution.py:154
  399.0 21.7 %collective-permute-done.24 = bf16[1,600,128]{2,1,0:T(8,128)(2,1)S(1)} collective-permute-done((bf16[1,600,128]{2,1,0:T(8,128)(2,1)S(1)}, bf16[1,600,128]{2,1,0:T(8,128)(2,1)S(1)}, u32[]{:S(2)}, u32[]{:S(2)}) %collective-permute-start.24) | collective-permute-done | bytes 153632 | tf_op jit(solution)/shard_map/ppermute | solution.py:92
  430.7 20.2 %fusion.2 = bf16[1792,128]{0,1:T(8,128)(2,1)S(1)} fusion(bf16[14400,128]{1,0:T(8,128)(2,1)} %fusion.29, bf16[14400,1792]{1,0:T(8,128)(2,1)} %bitcast.438), kind=kOutput, calls=%fused_computation.20 | convolution fusion | flops 6606258176 | bytes 55754752 | tf_op jit(solution)/shard_map/dot_general | solution.py:12
  451.9 4.5 all-to-all-start.4
  460.4 18.7 %all-to-all-done.4 = bf16[8,224,128]{2,1,0:T(8,128)(2,1)S(1)} async-done(((bf16[8,224,128]{2,1,0:T(8,128)(2,1)}), bf16[8,224,128]{2,1,0:T(8,128)(2,1)S(1)}, u32[]{:S(2)}, u32[]{:S(2)}) %all-to-all-start.4) | async-done | bytes 458784 | tf_op jit(solution)/shard_map/all_to_all | solution.py:130
  479.9 8.2 %all-to-all-start.5 = ((bf16[8,224,128]{2,1,0:T(8,128)(2,1)}), bf16[8,224,128]{2,1,0:T(8,128)(2,1)S(1)}, u32[]{:S(2)}, u32[]{:S(2)}) async-start(bf16[8,224,128]{2,1,0:T(8,128)(2,1)} %broadcast_in_dim.8), calls=%async_computation.5 | async-start | bytes 917504 | tf_op jit(solution)/shard_map/all_to_all | solution.py:135
  495.1 16.8 %all-to-all-done.5 = bf16[8,224,128]{2,1,0:T(8,128)(2,1)S(1)} async-done(((bf16[8,224,128]{2,1,0:T(8,128)(2,1)}), bf16[8,224,128]{2,1,0:T(8,128)(2,1)S(1)}, u32[]{:S(2)}, u32[]{:S(2)}) %all-to-all-start.5) | async-done | bytes 458784 | tf_op jit(solution)/shard_map/all_to_all | solution.py:135
  515.2 8.4 %shard_map.81 = f32[300,24,128]{2,1,0:T(8,128)S(1)} custom-call(bf16[2,300,640]{2,1,0:T(8,128)(2,1)S(1)} %copy.22.refs_0_, bf16[640,3072]{1,0:T(8,128)(2,1)S(1)} %copy-done.1), custom_call_target="tpu_custom_call" | custom-call | flops 2359296000 | bytes 7618560 | tf_op jit(solution)/shard_map/pallas_call | solution.py:187
  523.6 9.2 %shard_map.82 = f32[2400,128]{1,0:T(8,128)S(1)} custom-call(bf16[2,7200,1792]{2,1,0:T(8,128)(2,1)} %bitcast.439, bf16[1792,128]{1,0:T(8,128)(2,1)S(1)} %bitcast.405, bf16[1792,128]{1,0:T(8,128)(2,1)S(1)} %pad_maximum_fusion.16.turned_ref, f32[7200,128]{1,0:T(8,128)S(1)} %bitcast.391), custom_call_target="tpu_custom_call" | custom-call | flops 2202009600 | bytes 19660800 | tf_op jit(solution)/shard_map/pallas_call | solution.py:154
  532.9 9.3 %shard_map.83 = f32[2400,128]{1,0:T(8,128)S(1)} custom-call(bf16[2,7200,1792]{2,1,0:T(8,128)(2,1)} %bitcast.440, bf16[1792,128]{1,0:T(8,128)(2,1)S(1)} %bitcast.406, bf16[1792,128]{1,0:T(8,128)(2,1)S(1)} %pad_maximum_fusion.16.turned_ref, f32[7200,128]{1,0:T(8,128)S(1)} %bitcast.392), custom_call_target="tpu_custom_call" | custom-call | flops 2202009600 | bytes 19660800 | tf_op jit(solution)/shard_map/pallas_call | solution.py:154
  542.9 9.2 %shard_map.84 = f32[2400,128]{1,0:T(8,128)S(1)} custom-call(bf16[2,7200,1792]{2,1,0:T(8,128)(2,1)} %bitcast.441, bf16[1792,128]{1,0:T(8,128)(2,1)S(1)} %bitcast.407, bf16[1792,128]{1,0:T(8,128)(2,1)S(1)} %pad_maximum_fusion.16.turned_ref, f32[7200,128]{1,0:T(8,128)S(1)} %bitcast.393), custom_call_target="tpu_custom_call" | custom-call | flops 2202009600 | bytes 19660800 | tf_op jit(solution)/shard_map/pallas_call | solution.py:154
  555.5 3.8 collective-permute-done.28
  559.4 3.3 collective-permute-done.32
  568.7 4.1 collective-permute-done.37
  573.0 3.1 collective-permute-done.33
  580.4 4.2 fusion.148
  584.7 3.5 copy.37
  588.2 5.0 copy.36
  593.2 4.5 pad_maximum_fusion
  597.7 8.0 %copy.38 = f32[2,300,1536]{2,0,1:T(2,128)} copy(f32[2,300,1536]{1,2,0:T(8,128)} %pad_maximum_fusion) | data formatting | bytes 7372800 | tf_op jit(solution)/shard_map/stack | solution.py:285
  (342 shorter events, 143.5 us)
Async XLA Ops:
  6.5 152.7 %all-gather.4.cloned.1.call-start = ((), (), s32[]{:S(2)}) async-start(), calls=%async_computation.6 | async-start | bytes 4423680 | tf_op jit(solution)/shard_map/all_gather | solution.py:255
  39.3 5.9 collective-permute-start
  69.2 48.8 %all-to-all-start = ((bf16[8,224,128]{2,1,0:T(8,128)(2,1)}), bf16[8,224,128]{2,1,0:T(8,128)(2,1)S(1)}, u32[]{:S(2)}, u32[]{:S(2)}) async-start(bf16[8,224,128]{2,1,0:T(8,128)(2,1)} %bitcast.13), calls=%async_computation | async-start | bytes 917504 | tf_op jit(solution)/shard_map/all_to_all | solution.py:130
  119.0 35.2 %all-to-all-start.1 = ((bf16[8,224,128]{2,1,0:T(8,128)(2,1)}), bf16[8,224,128]{2,1,0:T(8,128)(2,1)S(1)}, u32[]{:S(2)}, u32[]{:S(2)}) async-start(bf16[8,224,128]{2,1,0:T(8,128)(2,1)} %broadcast_in_dim.6), calls=%async_computation.1 | async-start | bytes 917504 | tf_op jit(solution)/shard_map/all_to_all | solution.py:135
  127.3 210.9 %all-gather.6.cloned.1.call-start = ((), (), s32[]{:S(2)}) async-start(), calls=%async_computation.7 | async-start | bytes 4423680 | tf_op jit(solution)/shard_map/all_gather | solution.py:255
  188.3 10.1 %collective-permute-start.5 = (bf16[2,600,128]{2,1,0:T(8,128)(2,1)S(1)}, bf16[2,600,128]{2,1,0:T(8,128)(2,1)S(1)}, u32[]{:S(2)}, u32[]{:S(2)}) collective-permute-start(bf16[2,600,128]{2,1,0:T(8,128)(2,1)S(1)} %fusion.31), channel_id=1, source_target_pairs={{0,1},{1,0},{2,3},{3,2},{4,5},{5,4},{6,7},{7,6},{8,9},{9,8},{10,11... | collective-permute-start | bytes 921608 | tf_op jit(solution)/shard_map/ppermute | solution.py:92
  188.4 13.2 %collective-permute-start.1 = (bf16[2,600,128]{2,1,0:T(8,128)(2,1)S(1)}, bf16[2,600,128]{2,1,0:T(8,128)(2,1)S(1)}, u32[]{:S(2)}, u32[]{:S(2)}) collective-permute-start(bf16[2,600,128]{2,1,0:T(8,128)(2,1)S(1)} %fusion.30), channel_id=1, source_target_pairs={{0,1},{1,0},{2,3},{3,2},{4,5},{5,4},{6,7},{7,6},{8,9},{9,8},{10,11... | collective-permute-start | bytes 921608 | tf_op jit(solution)/shard_map/ppermute | solution.py:92
  198.3 3.5 collective-permute-start.9
  198.5 7.9 %collective-permute-start.6 = (bf16[1,600,128]{2,1,0:T(8,128)(2,1)S(1)}, bf16[1,600,128]{2,1,0:T(8,128)(2,1)S(1)}, u32[]{:S(2)}, u32[]{:S(2)}) collective-permute-start(bf16[1,600,128]{2,1,0:T(8,128)(2,1)S(1)} %dynamic-slice_convert_fusion.16), channel_id=1, source_target_pairs={{0,2},{1,3},{2,0},{3,1},{4,6},{5,7},{6,4},{7,5},{8,10},{9,11},{10,... | collective-permute-start | bytes 460808 | tf_op jit(solution)/shard_map/ppermute | solution.py:92
  201.7 8.0 %collective-permute-start.2 = (bf16[1,600,128]{2,1,0:T(8,128)(2,1)S(1)}, bf16[1,600,128]{2,1,0:T(8,128)(2,1)S(1)}, u32[]{:S(2)}, u32[]{:S(2)}) collective-permute-start(bf16[1,600,128]{2,1,0:T(8,128)(2,1)S(1)} %dynamic-slice_convert_fusion.17), channel_id=1, source_target_pairs={{0,2},{1,3},{2,0},{3,1},{4,6},{5,7},{6,4},{7,5},{8,10},{9,11},{10,... | collective-permute-start | bytes 460808 | tf_op jit(solution)/shard_map/ppermute | solution.py:92
  201.9 10.9 %collective-permute-start.10 = (bf16[1,600,128]{2,1,0:T(8,128)(2,1)S(1)}, bf16[1,600,128]{2,1,0:T(8,128)(2,1)S(1)}, u32[]{:S(2)}, u32[]{:S(2)}) collective-permute-start(bf16[1,600,128]{2,1,0:T(8,128)(2,1)S(1)} %dynamic-slice_convert_fusion.15), channel_id=1, source_target_pairs={{0,2},{1,3},{2,0},{3,1},{4,6},{5,7},{6,4},{7,5},{8,10},{9,11},{10,... | collective-permute-start | bytes 460808 | tf_op jit(solution)/shard_map/ppermute | solution.py:92
  214.2 6.9 %collective-permute-start.3 = (bf16[1,600,128]{2,1,0:T(8,128)(2,1)S(1)}, bf16[1,600,128]{2,1,0:T(8,128)(2,1)S(1)}, u32[]{:S(2)}, u32[]{:S(2)}) collective-permute-start(bf16[1,600,128]{2,1,0:T(8,128)(2,1)S(1)} %bitcast.489), channel_id=1, source_target_pairs={{0,2},{1,3},{2,0},{3,1},{4,6},{5,7},{6,4},{7,5},{8,10},{9,11},{10,... | collective-permute-start | bytes 460808 | tf_op jit(solution)/shard_map/ppermute | solution.py:92
  216.1 28.6 %collective-permute-start.7 = (bf16[1,600,128]{2,1,0:T(8,128)(2,1)S(1)}, bf16[1,600,128]{2,1,0:T(8,128)(2,1)S(1)}, u32[]{:S(2)}, u32[]{:S(2)}) collective-permute-start(bf16[1,600,128]{2,1,0:T(8,128)(2,1)S(1)} %bitcast.487), channel_id=1, source_target_pairs={{0,2},{1,3},{2,0},{3,1},{4,6},{5,7},{6,4},{7,5},{8,10},{9,11},{10,... | collective-permute-start | bytes 460808 | tf_op jit(solution)/shard_map/ppermute | solution.py:92
  216.3 30.4 %collective-permute-start.11 = (bf16[1,600,128]{2,1,0:T(8,128)(2,1)S(1)}, bf16[1,600,128]{2,1,0:T(8,128)(2,1)S(1)}, u32[]{:S(2)}, u32[]{:S(2)}) collective-permute-start(bf16[1,600,128]{2,1,0:T(8,128)(2,1)S(1)} %bitcast.485), channel_id=1, source_target_pairs={{0,2},{1,3},{2,0},{3,1},{4,6},{5,7},{6,4},{7,5},{8,10},{9,11},{10,... | collective-permute-start | bytes 460808 | tf_op jit(solution)/shard_map/ppermute | solution.py:92
  218.3 34.4 %collective-permute-start.13 = (bf16[80,3072]{1,0:T(8,128)(2,1)S(1)}, bf16[80,3072]{1,0:T(8,128)(2,1)}, u32[]{:S(2)}, u32[]{:S(2)}) collective-permute-start(bf16[80,3072]{1,0:T(8,128)(2,1)S(1)} %pad.16), channel_id=1, source_target_pairs={{0,0},{1,4},{2,8},{3,12},{4,16},{5,20},{6,24},{7,28},{8,1},{9,5},{... | collective-permute-start | bytes 1474568 | tf_op jit(solution)/shard_map/ppermute | solution.py:254
  221.3 25.6 %collective-permute-start.4 = (bf16[2,600,128]{2,1,0:T(8,128)(2,1)S(1)}, bf16[2,600,128]{2,1,0:T(8,128)(2,1)S(1)}, u32[]{:S(2)}, u32[]{:S(2)}) collective-permute-start(bf16[2,600,128]{2,1,0:T(8,128)(2,1)S(1)} %maximum_bitcast_fusion), channel_id=1, source_target_pairs={{0,1},{1,0},{2,3},{3,2},{4,5},{5,4},{6,7},{7,6},{8,9},{9,8},{10,11... | collective-permute-start | bytes 921608 | tf_op jit(solution)/shard_map/ppermute | solution.py:92
  244.7 3.4 collective-permute-start.8
  246.8 3.6 collective-permute-start.12
  277.9 29.0 %all-to-all-start.2 = ((bf16[8,224,128]{2,1,0:T(8,128)(2,1)}), bf16[8,224,128]{2,1,0:T(8,128)(2,1)S(1)}, u32[]{:S(2)}, u32[]{:S(2)}) async-start(bf16[8,224,128]{2,1,0:T(8,128)(2,1)} %bitcast.478), calls=%async_computation.2 | async-start | bytes 917504 | tf_op jit(solution)/shard_map/all_to_all | solution.py:130
  307.8 28.9 %all-to-all-start.3 = ((bf16[8,224,128]{2,1,0:T(8,128)(2,1)}), bf16[8,224,128]{2,1,0:T(8,128)(2,1)S(1)}, u32[]{:S(2)}, u32[]{:S(2)}) async-start(bf16[8,224,128]{2,1,0:T(8,128)(2,1)} %broadcast_in_dim.7), calls=%async_computation.3 | async-start | bytes 917504 | tf_op jit(solution)/shard_map/all_to_all | solution.py:135
  313.5 199.6 %all-gather.8.cloned.1.call-start = ((), (), s32[]{:S(2)}) async-start(), calls=%async_computation.8 | async-start | bytes 4423680 | tf_op jit(solution)/shard_map/all_gather | solution.py:255
  367.3 10.3 %collective-permute-start.14 = (bf16[2,600,128]{2,1,0:T(8,128)(2,1)S(1)}, bf16[2,600,128]{2,1,0:T(8,128)(2,1)S(1)}, u32[]{:S(2)}, u32[]{:S(2)}) collective-permute-start(bf16[2,600,128]{2,1,0:T(8,128)(2,1)S(1)} %fusion.33), channel_id=1, source_target_pairs={{0,1},{1,0},{2,3},{3,2},{4,5},{5,4},{6,7},{7,6},{8,9},{9,8},{10,11... | collective-permute-start | bytes 921608 | tf_op jit(solution)/shard_map/ppermute | solution.py:92
  367.4 11.9 %collective-permute-start.18 = (bf16[2,600,128]{2,1,0:T(8,128)(2,1)S(1)}, bf16[2,600,128]{2,1,0:T(8,128)(2,1)S(1)}, u32[]{:S(2)}, u32[]{:S(2)}) collective-permute-start(bf16[2,600,128]{2,1,0:T(8,128)(2,1)S(1)} %fusion.34), channel_id=1, source_target_pairs={{0,1},{1,0},{2,3},{3,2},{4,5},{5,4},{6,7},{7,6},{8,9},{9,8},{10,11... | collective-permute-start | bytes 921608 | tf_op jit(solution)/shard_map/ppermute | solution.py:92
  377.5 2.5 collective-permute-start.22
  377.7 6.9 %collective-permute-start.15 = (bf16[1,600,128]{2,1,0:T(8,128)(2,1)S(1)}, bf16[1,600,128]{2,1,0:T(8,128)(2,1)S(1)}, u32[]{:S(2)}, u32[]{:S(2)}) collective-permute-start(bf16[1,600,128]{2,1,0:T(8,128)(2,1)S(1)} %dynamic-slice_convert_fusion.14), channel_id=1, source_target_pairs={{0,2},{1,3},{2,0},{3,1},{4,6},{5,7},{6,4},{7,5},{8,10},{9,11},{10,... | collective-permute-start | bytes 460808 | tf_op jit(solution)/shard_map/ppermute | solution.py:92
  379.4 8.5 %collective-permute-start.19 = (bf16[1,600,128]{2,1,0:T(8,128)(2,1)S(1)}, bf16[1,600,128]{2,1,0:T(8,128)(2,1)S(1)}, u32[]{:S(2)}, u32[]{:S(2)}) collective-permute-start(bf16[1,600,128]{2,1,0:T(8,128)(2,1)S(1)} %dynamic-slice_convert_fusion.13), channel_id=1, source_target_pairs={{0,2},{1,3},{2,0},{3,1},{4,6},{5,7},{6,4},{7,5},{8,10},{9,11},{10,... | collective-permute-start | bytes 460808 | tf_op jit(solution)/shard_map/ppermute | solution.py:92
  380.0 11.1 %collective-permute-start.23 = (bf16[1,600,128]{2,1,0:T(8,128)(2,1)S(1)}, bf16[1,600,128]{2,1,0:T(8,128)(2,1)S(1)}, u32[]{:S(2)}, u32[]{:S(2)}) collective-permute-start(bf16[1,600,128]{2,1,0:T(8,128)(2,1)S(1)} %dynamic-slice_convert_fusion.12), channel_id=1, source_target_pairs={{0,2},{1,3},{2,0},{3,1},{4,6},{5,7},{6,4},{7,5},{8,10},{9,11},{10,... | collective-permute-start | bytes 460808 | tf_op jit(solution)/shard_map/ppermute | solution.py:92
  385.4 11.2 %collective-permute-start.16 = (bf16[1,600,128]{2,1,0:T(8,128)(2,1)S(1)}, bf16[1,600,128]{2,1,0:T(8,128)(2,1)S(1)}, u32[]{:S(2)}, u32[]{:S(2)}) collective-permute-start(bf16[1,600,128]{2,1,0:T(8,128)(2,1)S(1)} %bitcast.479), channel_id=1, source_target_pairs={{0,2},{1,3},{2,0},{3,1},{4,6},{5,7},{6,4},{7,5},{8,10},{9,11},{10,... | collective-permute-start | bytes 460808 | tf_op jit(solution)/shard_map/ppermute | solution.py:92
  388.6 10.2 %collective-permute-start.20 = (bf16[1,600,128]{2,1,0:T(8,128)(2,1)S(1)}, bf16[1,600,128]{2,1,0:T(8,128)(2,1)S(1)}, u32[]{:S(2)}, u32[]{:S(2)}) collective-permute-start(bf16[1,600,128]{2,1,0:T(8,128)(2,1)S(1)} %bitcast.481), channel_id=1, source_target_pairs={{0,2},{1,3},{2,0},{3,1},{4,6},{5,7},{6,4},{7,5},{8,10},{9,11},{10,... | collective-permute-start | bytes 460808 | tf_op jit(solution)/shard_map/ppermute | solution.py:92
  391.9 28.8 %collective-permute-start.24 = (bf16[1,600,128]{2,1,0:T(8,128)(2,1)S(1)}, bf16[1,600,128]{2,1,0:T(8,128)(2,1)S(1)}, u32[]{:S(2)}, u32[]{:S(2)}) collective-permute-start(bf16[1,600,128]{2,1,0:T(8,128)(2,1)S(1)} %bitcast.483), channel_id=1, source_target_pairs={{0,2},{1,3},{2,0},{3,1},{4,6},{5,7},{6,4},{7,5},{8,10},{9,11},{10,... | collective-permute-start | bytes 460808 | tf_op jit(solution)/shard_map/ppermute | solution.py:92
  393.8 33.0 %collective-permute-start.26 = (bf16[80,3072]{1,0:T(8,128)(2,1)S(1)}, bf16[80,3072]{1,0:T(8,128)(2,1)}, u32[]{:S(2)}, u32[]{:S(2)}) collective-permute-start(bf16[80,3072]{1,0:T(8,128)(2,1)S(1)} %pad.17), channel_id=1, source_target_pairs={{0,0},{1,4},{2,8},{3,12},{4,16},{5,20},{6,24},{7,28},{8,1},{9,5},{... | collective-permute-start | bytes 1474568 | tf_op jit(solution)/shard_map/ppermute | solution.py:254
  396.7 24.2 %collective-permute-start.17 = (bf16[2,600,128]{2,1,0:T(8,128)(2,1)S(1)}, bf16[2,600,128]{2,1,0:T(8,128)(2,1)S(1)}, u32[]{:S(2)}, u32[]{:S(2)}) collective-permute-start(bf16[2,600,128]{2,1,0:T(8,128)(2,1)S(1)} %maximum_bitcast_fusion.3), channel_id=1, source_target_pairs={{0,1},{1,0},{2,3},{3,2},{4,5},{5,4},{6,7},{7,6},{8,9},{9,8},{10,11... | collective-permute-start | bytes 921608 | tf_op jit(solution)/shard_map/ppermute | solution.py:92
  398.9 23.3 %collective-permute-start.21 = (bf16[2,600,128]{2,1,0:T(8,128)(2,1)S(1)}, bf16[2,600,128]{2,1,0:T(8,128)(2,1)S(1)}, u32[]{:S(2)}, u32[]{:S(2)}) collective-permute-start(bf16[2,600,128]{2,1,0:T(8,128)(2,1)S(1)} %maximum_bitcast_fusion.4), channel_id=1, source_target_pairs={{0,1},{1,0},{2,3},{3,2},{4,5},{5,4},{6,7},{7,6},{8,9},{9,8},{10,11... | collective-permute-start | bytes 921608 | tf_op jit(solution)/shard_map/ppermute | solution.py:92
  420.8 3.7 collective-permute-start.25
  451.9 27.2 %all-to-all-start.4 = ((bf16[8,224,128]{2,1,0:T(8,128)(2,1)}), bf16[8,224,128]{2,1,0:T(8,128)(2,1)S(1)}, u32[]{:S(2)}, u32[]{:S(2)}) async-start(bf16[8,224,128]{2,1,0:T(8,128)(2,1)} %bitcast.477), calls=%async_computation.4 | async-start | bytes 917504 | tf_op jit(solution)/shard_map/all_to_all | solution.py:130
  479.9 32.1 %all-to-all-start.5 = ((bf16[8,224,128]{2,1,0:T(8,128)(2,1)}), bf16[8,224,128]{2,1,0:T(8,128)(2,1)S(1)}, u32[]{:S(2)}, u32[]{:S(2)}) async-start(bf16[8,224,128]{2,1,0:T(8,128)(2,1)} %broadcast_in_dim.8), calls=%async_computation.5 | async-start | bytes 917504 | tf_op jit(solution)/shard_map/all_to_all | solution.py:135
  542.2 10.1 %collective-permute-start.27 = (bf16[2,600,128]{2,1,0:T(8,128)(2,1)S(1)}, bf16[2,600,128]{2,1,0:T(8,128)(2,1)S(1)}, u32[]{:S(2)}, u32[]{:S(2)}) collective-permute-start(bf16[2,600,128]{2,1,0:T(8,128)(2,1)S(1)} %fusion.36), channel_id=1, source_target_pairs={{0,1},{1,0},{2,3},{3,2},{4,5},{5,4},{6,7},{7,6},{8,9},{9,8},{10,11... | collective-permute-start | bytes 921608 | tf_op jit(solution)/shard_map/ppermute | solution.py:92
  542.3 10.9 %collective-permute-start.31 = (bf16[2,600,128]{2,1,0:T(8,128)(2,1)S(1)}, bf16[2,600,128]{2,1,0:T(8,128)(2,1)S(1)}, u32[]{:S(2)}, u32[]{:S(2)}) collective-permute-start(bf16[2,600,128]{2,1,0:T(8,128)(2,1)S(1)} %fusion.37), channel_id=1, source_target_pairs={{0,1},{1,0},{2,3},{3,2},{4,5},{5,4},{6,7},{7,6},{8,9},{9,8},{10,11... | collective-permute-start | bytes 921608 | tf_op jit(solution)/shard_map/ppermute | solution.py:92
  552.2 2.5 collective-permute-start.35
  552.4 6.9 %collective-permute-start.28 = (bf16[1,600,128]{2,1,0:T(8,128)(2,1)S(1)}, bf16[1,600,128]{2,1,0:T(8,128)(2,1)S(1)}, u32[]{:S(2)}, u32[]{:S(2)}) collective-permute-start(bf16[1,600,128]{2,1,0:T(8,128)(2,1)S(1)} %dynamic-slice_convert_fusion.11), channel_id=1, source_target_pairs={{0,2},{1,3},{2,0},{3,1},{4,6},{5,7},{6,4},{7,5},{8,10},{9,11},{10,... | collective-permute-start | bytes 460808 | tf_op jit(solution)/shard_map/ppermute | solution.py:92
  553.3 9.4 %collective-permute-start.32 = (bf16[1,600,128]{2,1,0:T(8,128)(2,1)S(1)}, bf16[1,600,128]{2,1,0:T(8,128)(2,1)S(1)}, u32[]{:S(2)}, u32[]{:S(2)}) collective-permute-start(bf16[1,600,128]{2,1,0:T(8,128)(2,1)S(1)} %dynamic-slice_convert_fusion.10), channel_id=1, source_target_pairs={{0,2},{1,3},{2,0},{3,1},{4,6},{5,7},{6,4},{7,5},{8,10},{9,11},{10,... | collective-permute-start | bytes 460808 | tf_op jit(solution)/shard_map/ppermute | solution.py:92
  554.8 10.7 %collective-permute-start.36 = (bf16[1,600,128]{2,1,0:T(8,128)(2,1)S(1)}, bf16[1,600,128]{2,1,0:T(8,128)(2,1)S(1)}, u32[]{:S(2)}, u32[]{:S(2)}) collective-permute-start(bf16[1,600,128]{2,1,0:T(8,128)(2,1)S(1)} %dynamic-slice_convert_fusion.9), channel_id=1, source_target_pairs={{0,2},{1,3},{2,0},{3,1},{4,6},{5,7},{6,4},{7,5},{8,10},{9,11},{10,... | collective-permute-start | bytes 460808 | tf_op jit(solution)/shard_map/ppermute | solution.py:92
  565.9 6.9 %collective-permute-start.37 = (bf16[1,600,128]{2,1,0:T(8,128)(2,1)S(1)}, bf16[1,600,128]{2,1,0:T(8,128)(2,1)S(1)}, u32[]{:S(2)}, u32[]{:S(2)}) collective-permute-start(bf16[1,600,128]{2,1,0:T(8,128)(2,1)S(1)} %bitcast.504), channel_id=1, source_target_pairs={{0,2},{1,3},{2,0},{3,1},{4,6},{5,7},{6,4},{7,5},{8,10},{9,11},{10,... | collective-permute-start | bytes 460808 | tf_op jit(solution)/shard_map/ppermute | solution.py:92
  566.7 9.4 %collective-permute-start.33 = (bf16[1,600,128]{2,1,0:T(8,128)(2,1)S(1)}, bf16[1,600,128]{2,1,0:T(8,128)(2,1)S(1)}, u32[]{:S(2)}, u32[]{:S(2)}) collective-permute-start(bf16[1,600,128]{2,1,0:T(8,128)(2,1)S(1)} %bitcast.502), channel_id=1, source_target_pairs={{0,2},{1,3},{2,0},{3,1},{4,6},{5,7},{6,4},{7,5},{8,10},{9,11},{10,... | collective-permute-start | bytes 460808 | tf_op jit(solution)/shard_map/ppermute | solution.py:92
  568.0 10.1 %collective-permute-start.29 = (bf16[1,600,128]{2,1,0:T(8,128)(2,1)S(1)}, bf16[1,600,128]{2,1,0:T(8,128)(2,1)S(1)}, u32[]{:S(2)}, u32[]{:S(2)}) collective-permute-start(bf16[1,600,128]{2,1,0:T(8,128)(2,1)S(1)} %bitcast.500), channel_id=1, source_target_pairs={{0,2},{1,3},{2,0},{3,1},{4,6},{5,7},{6,4},{7,5},{8,10},{9,11},{10,... | collective-permute-start | bytes 460808 | tf_op jit(solution)/shard_map/ppermute | solution.py:92
  572.9 5.3 collective-permute-start.38
  576.2 2.1 collective-permute-start.34
  578.2 1.7 collective-permute-start.30
  (46 other events, 370.2 us)
Sparse Core Ops, SparseCore 0:
  46.1 113.0 all-gather.3
  252.9 85.2 all-gather.5
  426.9 86.1 all-gather.7

commit v2 on v1

--- a/solution.py
+++ b/solution.py
@@ -78,7 +78,7 @@
     return amplitude
 
 
-ROW_CHUNKS = 3
+ROW_CHUNKS = 1
 ROW_TILE = 512
 VIR_TILE = 16
 
@@ -280,6 +280,8 @@
             )
         amplitude = updated
         own_rounded = [a.astype(jnp.bfloat16) for a in amplitude]
+        if not last:
+            gathered, own_rounded = lax.optimization_barrier((gathered, own_rounded))
     change = jnp.concatenate(gathered).reshape(local_vir, active, lanes).astype(jnp.float32)
     result = start + change
     return jnp.stack([result[..., :pairs], result[..., pairs:]]).reshape(source.shape)

time: 621 us -> 664 us (1.069)
  blocking collectives: 0 us -> 218 us
  starting transfers between devices: 99.2 us -> 19 us
  waiting for transfers between devices: 181 us -> 106 us
  matrix products: 87.3 us -> 71.4 us
  Pallas kernels: 108 us -> 100 us
  local copies, waits for them, and re-layouts: 73.8 us -> 80.8 us
    all_to_all x0 -> x5, blocking collectives: none -> 218 us  [the longest x3 152 us: vir_sum(): lax.all_to_all(values.astype(jnp.bfloat16).reshape(size, rows // size, la...]
    all_to_all x3 -> x0, waiting for transfers between devices: 46.5 us -> none  [vir_sum(): lax.all_to_all(values.astype(jnp.bfloat16).reshape(size, rows // size, la...]
    all_to_all x3 -> x0, starting transfers between devices: 42.4 us -> none  [vir_sum(): lax.all_to_all(values.astype(jnp.bfloat16).reshape(size, rows // size, la...]
    all_to_all x3 -> x1, waiting for transfers between devices: 47.8 us -> 22.5 us  [vir_sum(): return lax.all_to_all(spread, 'vir', 0, 0).reshape(rows, lanes)]
    ppermute x36 -> x12, starting transfers between devices: 29.6 us -> 7.85 us  [swap(): return lax.ppermute(values, 'fit', [(i, i ^ bit) for i in range(size)])]
    all_to_all x3 -> x1, starting transfers between devices: 22.3 us -> 8.48 us  [vir_sum(): return lax.all_to_all(spread, 'vir', 0, 0).reshape(rows, lanes)]
    dot_general x9 -> x3, matrix products: 12.8 us -> 2.79 us  [per_device(): jnp.einsum('aul,ut->atl', value, actfock[0], precision=highest)]
    unnamed x6 -> x0, other arithmetic: 9.75 us -> none
  transfers between devices with their start and end apart: 48 -> 19, of which waited for: 26 -> 15; matrix products, arithmetic and copies ran while one was open for 23% -> 16% of each run, Pallas kernels for 5% -> 0%
where the time goes in v2:
time: 664 us; the launch traced here: 655 us
  blocking collectives  218 us (33%)
  waiting for transfers between devices  106 us (16%)
  Pallas kernels  100 us (15%)
  local copies, waits for them, and re-layouts  80.8 us (12%)
  matrix products  71.4 us (11%)
  other arithmetic  45.9 us (7%)
  starting transfers between devices  19 us (3%)
  between operations  14.4 us (2%)
    all_to_all x3, blocking collectives, vir_sum(): lax.all_to_all(values.astype(jnp.bfloat16).reshape(size, rows // size, la...  152 us
    ppermute x12, waiting for transfers between devices, swap(): return lax.ppermute(values, 'fit', [(i, i ^ bit) for i in range(size)])  75.3 us
    pallas_call x3, Pallas kernels, back_product(): pl.pallas_call(back_kernel, grid=(rows // tile,), in_specs=[pl.BlockSpec(...  75.2 us
    all_to_all x2, blocking collectives, vir_sum(): return lax.all_to_all(spread, 'vir', 0, 0).reshape(rows, lanes)  66.3 us
    dot_general x3, matrix products, contract_first(): lax.dot_general(left, right, (((0,), (0,)), ((), ())), preferred_element_...  63.3 us
    pallas_call x3, Pallas kernels, virtual_product(): pl.pallas_call(lambda *refs: virtual_kernel(pairs, *refs), grid=(active /...  25.1 us
    unnamed x64, local copies, waits for them, and re-layouts  23.9 us
    all_to_all x1, waiting for transfers between devices, vir_sum(): return lax.all_to_all(spread, 'vir', 0, 0).reshape(rows, lanes)  22.5 us
  transfers between devices with their start and end apart: 19, of which 15 were waited for; matrix products, arithmetic and copies ran while one was open for 16% of the time, Pallas kernels for 0%

profile of v2, /device:TPU:0, one launch (start us, length us, event | category | flops | bytes accessed | tf_op | source)
XLA Modules:
  0.0 655.4 jit_solution(11834919173570954754)
XLA Ops:
  6.5 7.7 %fusion.80 = (f32[1,300,1536]{2,0,1:T(1,128)S(1)}, f32[1,300,1536]{2,0,1:T(1,128)}) fusion(f32[2,300,1536]{2,0,1:T(2,128)} %param.13), kind=kLoop, calls=%fused_computation.128 | loop fusion | bytes 7372800 | tf_op jit(solution)/shard_map/slice | solution.py:220
  14.2 5.2 copy.36
  19.4 4.8 copy.16
  24.2 3.4 copy.35
  27.6 4.9 copy.15
  32.7 2.7 broadcast_subtract_fusion.1
  35.4 7.2 %maximum_divide_fusion = f32[300,24,128]{2,1,0:T(8,128)S(1)} fusion(f32[300,24,64]{2,1,0:T(8,128)} %copy.16, f32[300,24,64]{2,1,0:T(8,128)} %copy.15, f32[300,24,64]{2,1,0:T(8,128)} %broadcast_subtract_fusion.1), kind=kLoop, calls=%fused_computation.1 | loop fusion | flops 2764800 | bytes 9216000 | tf_op jit(solution)/shard_map/div | solution.py:221
  48.4 4.2 concatenate.57
  52.6 2.6 concatenate.56
  57.3 4.0 fusion
  64.0 22.8 %fusion.22 = bf16[1792,128]{0,1:T(8,128)(2,1)S(1)} fusion(bf16[14400,1792]{1,0:T(8,128)(2,1)} %bitcast.173, bf16[7200,128]{1,0:T(8,128)(2,1)S(1)} %maximum_negate_fusion, bf16[7200,128]{1,0:T(8,128)(2,1)S(1)} %fusion), kind=kOutput, calls=%fused_computation.23 | convolution fusion | flops 6613630976 | bytes 55754752 | tf_op jit(solution)/shard_map/dot_general | solution.py:12
  87.1 38.3 %all_to_all.30 = bf16[8,224,128]{2,1,0:T(8,128)(2,1)S(1)} all-to-all(bf16[8,224,128]{2,1,0:T(8,128)(2,1)S(1)} %bitcast.205), channel_id=1, replica_groups=mesh['vir'=8,'fit'=4] {'vir'}, dimensions={0} | all-to-all | bytes 917504 | tf_op jit(solution)/shard_map/all_to_all | solution.py:130
  126.3 8.5 %all-to-all-start.1 = ((bf16[8,224,128]{2,1,0:T(8,128)(2,1)}), bf16[8,224,128]{2,1,0:T(8,128)(2,1)S(1)}, u32[]{:S(2)}, u32[]{:S(2)}) async-start(bf16[8,224,128]{2,1,0:T(8,128)(2,1)} %broadcast_in_dim.6), calls=%async_computation.1 | async-start | bytes 917504 | tf_op jit(solution)/shard_map/all_to_all | solution.py:135
  138.1 22.5 %all-to-all-done.1 = bf16[8,224,128]{2,1,0:T(8,128)(2,1)S(1)} async-done(((bf16[8,224,128]{2,1,0:T(8,128)(2,1)}), bf16[8,224,128]{2,1,0:T(8,128)(2,1)S(1)}, u32[]{:S(2)}, u32[]{:S(2)}) %all-to-all-start.1) | async-done | bytes 458784 | tf_op jit(solution)/shard_map/all_to_all | solution.py:135
  161.0 3.2 all-gather.4.cloned.1.call-done.refs_1_
  166.4 8.4 %shard_map.73 = f32[300,24,128]{2,1,0:T(8,128)S(1)} custom-call(bf16[2,300,640]{2,1,0:T(8,128)(2,1)S(1)} %copy.24.refs_0_, bf16[640,3072]{1,0:T(8,128)(2,1)S(1)} %copy-done.2), custom_call_target="tpu_custom_call" | custom-call | flops 2359296000 | bytes 7618560 | tf_op jit(solution)/shard_map/pallas_call | solution.py:187
  174.8 25.1 %shard_map.74 = f32[7200,128]{1,0:T(8,128)S(1)} custom-call(bf16[2,7200,1792]{2,1,0:T(8,128)(2,1)} %bitcast.174, bf16[1792,128]{1,0:T(8,128)(2,1)S(1)} %bitcast.165, bf16[1792,128]{1,0:T(8,128)(2,1)S(1)} %pad_maximum_fusion.3.turned_ref, f32[7200,128]{1,0:T(8,128)S(1)} %bitcast.171), custom_call_target="tpu_custom_call" | custom-call | flops 6606028800 | bytes 58982400 | tf_op jit(solution)/shard_map/pallas_call | solution.py:154
  202.8 2.8 fusion.40
  207.6 3.0 collective-permute-start.2
  212.2 9.6 %collective-permute-done.2 = bf16[1,1800,128]{2,1,0:T(8,128)(2,1)S(1)} collective-permute-done((bf16[1,1800,128]{2,1,0:T(8,128)(2,1)S(1)}, bf16[1,1800,128]{2,1,0:T(8,128)(2,1)S(1)}, u32[]{:S(2)}, u32[]{:S(2)}) %collective-permute-start.2) | collective-permute-done | bytes 460832 | tf_op jit(solution)/shard_map/ppermute | solution.py:92
  224.0 10.8 %collective-permute-done.3 = bf16[1,1800,128]{2,1,0:T(8,128)(2,1)} collective-permute-done((bf16[1,1800,128]{2,1,0:T(8,128)(2,1)S(1)}, bf16[1,1800,128]{2,1,0:T(8,128)(2,1)}, u32[]{:S(2)}, u32[]{:S(2)}) %collective-permute-start.3) | collective-permute-done | bytes 460832 | tf_op jit(solution)/shard_map/ppermute | solution.py:92
  237.8 2.8 collective-permute-done.4
  245.5 2.8 slice_negate_fusion.2
  250.8 20.2 %fusion.25 = bf16[1792,128]{0,1:T(8,128)(2,1)S(1)} fusion(bf16[14400,1792]{1,0:T(8,128)(2,1)} %bitcast.175, bf16[7200,128]{1,0:T(8,128)(2,1)} %maximum_negate_fusion.1, bf16[7200,128]{1,0:T(8,128)(2,1)S(1)} %bitcast.180), kind=kOutput, calls=%fused_computation.24 | convolution fusion | flops 6613630976 | bytes 55754752 | tf_op jit(solution)/shard_map/dot_general | solution.py:12
  271.3 56.8 %all_to_all.31 = bf16[8,224,128]{2,1,0:T(8,128)(2,1)S(1)} all-to-all(bf16[8,224,128]{2,1,0:T(8,128)(2,1)S(1)} %bitcast.206), channel_id=1, replica_groups=mesh['vir'=8,'fit'=4] {'vir'}, dimensions={0} | all-to-all | bytes 917504 | tf_op jit(solution)/shard_map/all_to_all | solution.py:130
  328.2 33.3 %all_to_all.32 = bf16[8,224,128]{2,1,0:T(8,128)(2,1)S(1)} all-to-all(bf16[8,224,128]{2,1,0:T(8,128)(2,1)S(1)} %broadcast_in_dim.7), channel_id=1, replica_groups=mesh['vir'=8,'fit'=4] {'vir'}, dimensions={0} | all-to-all | bytes 917504 | tf_op jit(solution)/shard_map/all_to_all | solution.py:135
  361.9 2.8 all-gather.6.cloned.1.call-done.refs_1_
  366.9 8.4 %shard_map.75 = f32[300,24,128]{2,1,0:T(8,128)S(1)} custom-call(bf16[2,300,640]{2,1,0:T(8,128)(2,1)S(1)} %copy.24.refs_0_, bf16[640,3072]{1,0:T(8,128)(2,1)S(1)} %copy-done.3), custom_call_target="tpu_custom_call" | custom-call | flops 2359296000 | bytes 7618560 | tf_op jit(solution)/shard_map/pallas_call | solution.py:187
  375.3 25.1 %shard_map.76 = f32[7200,128]{1,0:T(8,128)S(1)} custom-call(bf16[2,7200,1792]{2,1,0:T(8,128)(2,1)} %bitcast.176, bf16[1792,128]{1,0:T(8,128)(2,1)S(1)} %bitcast.169, bf16[1792,128]{1,0:T(8,128)(2,1)S(1)} %pad_maximum_fusion.4.turned_ref, f32[7200,128]{1,0:T(8,128)S(1)} %bitcast.172), custom_call_target="tpu_custom_call" | custom-call | flops 6606028800 | bytes 58982400 | tf_op jit(solution)/shard_map/pallas_call | solution.py:154
  400.6 2.5 collective-permute-done.6
  405.6 10.4 %collective-permute-done.7 = bf16[1,1800,128]{2,1,0:T(8,128)(2,1)S(1)} collective-permute-done((bf16[1,1800,128]{2,1,0:T(8,128)(2,1)S(1)}, bf16[1,1800,128]{2,1,0:T(8,128)(2,1)S(1)}, u32[]{:S(2)}, u32[]{:S(2)}) %collective-permute-start.7) | collective-permute-done | bytes 460832 | tf_op jit(solution)/shard_map/ppermute | solution.py:92
  416.1 2.7 fusion.81
  419.8 10.9 %collective-permute-done.8 = bf16[1,1800,128]{2,1,0:T(8,128)(2,1)S(1)} collective-permute-done((bf16[1,1800,128]{2,1,0:T(8,128)(2,1)S(1)}, bf16[1,1800,128]{2,1,0:T(8,128)(2,1)S(1)}, u32[]{:S(2)}, u32[]{:S(2)}) %collective-permute-start.8) | collective-permute-done | bytes 460832 | tf_op jit(solution)/shard_map/ppermute | solution.py:92
  431.0 2.5 collective-permute-done.9
  437.1 2.8 slice_negate_fusion.1
  442.3 20.2 %fusion.28 = bf16[1792,128]{0,1:T(8,128)(2,1)S(1)} fusion(bf16[14400,1792]{1,0:T(8,128)(2,1)} %bitcast.177, bf16[7200,128]{1,0:T(8,128)(2,1)} %maximum_negate_fusion.2, bf16[7200,128]{1,0:T(8,128)(2,1)S(1)} %bitcast.182), kind=kOutput, calls=%fused_computation.25 | convolution fusion | flops 6613630976 | bytes 55754752 | tf_op jit(solution)/shard_map/dot_general | solution.py:12
  462.8 56.6 %all_to_all.33 = bf16[8,224,128]{2,1,0:T(8,128)(2,1)S(1)} all-to-all(bf16[8,224,128]{2,1,0:T(8,128)(2,1)S(1)} %bitcast.207), channel_id=1, replica_groups=mesh['vir'=8,'fit'=4] {'vir'}, dimensions={0} | all-to-all | bytes 917504 | tf_op jit(solution)/shard_map/all_to_all | solution.py:130
  520.9 33.0 %all_to_all.34 = bf16[8,224,128]{2,1,0:T(8,128)(2,1)S(1)} all-to-all(bf16[8,224,128]{2,1,0:T(8,128)(2,1)S(1)} %broadcast_in_dim.8), channel_id=1, replica_groups=mesh['vir'=8,'fit'=4] {'vir'}, dimensions={0} | all-to-all | bytes 917504 | tf_op jit(solution)/shard_map/all_to_all | solution.py:135
  558.2 8.4 %shard_map.77 = f32[300,24,128]{2,1,0:T(8,128)S(1)} custom-call(bf16[2,300,640]{2,1,0:T(8,128)(2,1)S(1)} %copy.24.refs_0_, bf16[640,3072]{1,0:T(8,128)(2,1)S(1)} %copy-done.4), custom_call_target="tpu_custom_call" | custom-call | flops 2359296000 | bytes 7618560 | tf_op jit(solution)/shard_map/pallas_call | solution.py:187
  566.5 25.1 %shard_map.78 = f32[7200,128]{1,0:T(8,128)S(1)} custom-call(bf16[2,7200,1792]{2,1,0:T(8,128)(2,1)} %bitcast.178, bf16[1792,128]{1,0:T(8,128)(2,1)S(1)} %bitcast.167, bf16[1792,128]{1,0:T(8,128)(2,1)S(1)} %pad_maximum_fusion.5.turned_ref, f32[7200,128]{1,0:T(8,128)S(1)} %bitcast.170), custom_call_target="tpu_custom_call" | custom-call | flops 6606028800 | bytes 58982400 | tf_op jit(solution)/shard_map/pallas_call | solution.py:154
  597.3 9.9 %collective-permute-done.12 = bf16[1,1800,128]{2,1,0:T(8,128)(2,1)S(1)} collective-permute-done((bf16[1,1800,128]{2,1,0:T(8,128)(2,1)S(1)}, bf16[1,1800,128]{2,1,0:T(8,128)(2,1)S(1)}, u32[]{:S(2)}, u32[]{:S(2)}) %collective-permute-start.12) | collective-permute-done | bytes 460832 | tf_op jit(solution)/shard_map/ppermute | solution.py:92
  608.1 11.4 %collective-permute-done.13 = bf16[1,1800,128]{2,1,0:T(8,128)(2,1)S(1)} collective-permute-done((bf16[1,1800,128]{2,1,0:T(8,128)(2,1)S(1)}, bf16[1,1800,128]{2,1,0:T(8,128)(2,1)S(1)}, u32[]{:S(2)}, u32[]{:S(2)}) %collective-permute-start.13) | collective-permute-done | bytes 460832 | tf_op jit(solution)/shard_map/ppermute | solution.py:92
  619.8 2.5 collective-permute-done.14
  623.3 4.2 fusion.79
  627.5 3.5 copy.33
  631.0 4.9 copy.32
  636.0 4.4 pad_maximum_fusion
  640.4 8.0 %copy.34 = f32[2,300,1536]{2,0,1:T(2,128)} copy(f32[2,300,1536]{1,2,0:T(8,128)} %pad_maximum_fusion) | data formatting | bytes 7372800 | tf_op jit(solution)/shard_map/stack | solution.py:287
  (158 shorter events, 63.3 us)
Async XLA Ops:
  6.5 157.7 %all-gather.4.cloned.1.call-start = ((), (), s32[]{:S(2)}) async-start(), calls=%async_computation.6 | async-start | bytes 4423680 | tf_op jit(solution)/shard_map/all_gather | solution.py:255
  27.6 5.0 copy-start.25
  27.6 5.0 copy-start.27
  27.6 5.1 copy-start.26
  42.6 4.2 copy-start.5
  42.7 2.8 copy-start.11
  42.9 18.3 %collective-permute-start = (bf16[80,3072]{1,0:T(8,128)(2,1)S(1)}, bf16[80,3072]{1,0:T(8,128)(2,1)S(1)}, u32[]{:S(2)}, u32[]{:S(2)}) collective-permute-start(bf16[80,3072]{1,0:T(8,128)(2,1)S(1)} %pad.15), channel_id=1, source_target_pairs={{0,0},{1,4},{2,8},{3,12},{4,16},{5,20},{6,24},{7,28},{8,1},{9,5},{... | collective-permute-start | bytes 1474568 | tf_op jit(solution)/shard_map/ppermute | solution.py:254
  48.3 4.3 copy-start.16
  55.2 2.0 copy-start.12
  61.3 0.8 copy-start.19
  126.3 34.3 %all-to-all-start.1 = ((bf16[8,224,128]{2,1,0:T(8,128)(2,1)}), bf16[8,224,128]{2,1,0:T(8,128)(2,1)S(1)}, u32[]{:S(2)}, u32[]{:S(2)}) async-start(bf16[8,224,128]{2,1,0:T(8,128)(2,1)} %broadcast_in_dim.6), calls=%async_computation.1 | async-start | bytes 917504 | tf_op jit(solution)/shard_map/all_to_all | solution.py:135
  134.8 230.0 %all-gather.6.cloned.1.call-start = ((), (), s32[]{:S(2)}) async-start(), calls=%async_computation.7 | async-start | bytes 4423680 | tf_op jit(solution)/shard_map/all_gather | solution.py:255
  164.3 2.1 copy-start.2
  199.9 1.8 copy-start
  202.8 4.1 collective-permute-start.1
  202.8 3.2 copy-start.6
  202.8 3.2 copy-start.22
  202.8 4.5 copy-start.1
  205.9 4.9 copy-start.13
  207.6 14.2 %collective-permute-start.2 = (bf16[1,1800,128]{2,1,0:T(8,128)(2,1)S(1)}, bf16[1,1800,128]{2,1,0:T(8,128)(2,1)S(1)}, u32[]{:S(2)}, u32[]{:S(2)}) collective-permute-start(bf16[1,1800,128]{2,1,0:T(8,128)(2,1)S(1)} %dynamic-slice_convert_fusion.5), channel_id=1, source_target_pairs={{0,2},{1,3},{2,0},{3,1},{4,6},{5,7},{6,4},{7,5},{8,10},{9,11},{10,... | collective-permute-start | bytes 1382408 | tf_op jit(solution)/shard_map/ppermute | solution.py:92
  222.1 183.1 %copy-start.10 = (f32[75,24,128]{2,1,0:T(8,128)}, f32[75,24,128]{2,1,0:T(8,128)S(1)}, u32[]{:S(2)}) copy-start(f32[75,24,128]{2,1,0:T(8,128)S(1)} %get-tuple-element.14) | copy-start | bytes 2764804
  222.2 12.6 %collective-permute-start.3 = (bf16[1,1800,128]{2,1,0:T(8,128)(2,1)S(1)}, bf16[1,1800,128]{2,1,0:T(8,128)(2,1)}, u32[]{:S(2)}, u32[]{:S(2)}) collective-permute-start(bf16[1,1800,128]{2,1,0:T(8,128)(2,1)S(1)} %bitcast.190), channel_id=1, source_target_pairs={{0,2},{1,3},{2,0},{3,1},{4,6},{5,7},{6,4},{7,5},{8,10},{9,11},{10,... | collective-permute-start | bytes 1382408 | tf_op jit(solution)/shard_map/ppermute | solution.py:92
  236.0 0.8 copy-start.17
  236.0 1.8 copy-start.18
  237.8 2.8 collective-permute-start.4
  243.8 0.7 collective-permute-start.5
  244.5 0.8 copy-start.20
  245.3 310.7 %all-gather.8.cloned.1.call-start = ((), (), s32[]{:S(2)}) async-start(), calls=%async_computation.8 | async-start | bytes 4423680 | tf_op jit(solution)/shard_map/all_gather | solution.py:255
  248.4 2.4 copy-start.8
  364.8 2.1 copy-start.3
  400.4 4.0 copy-start.23
  400.5 2.5 collective-permute-start.6
  403.3 12.7 %collective-permute-start.7 = (bf16[1,1800,128]{2,1,0:T(8,128)(2,1)S(1)}, bf16[1,1800,128]{2,1,0:T(8,128)(2,1)S(1)}, u32[]{:S(2)}, u32[]{:S(2)}) collective-permute-start(bf16[1,1800,128]{2,1,0:T(8,128)(2,1)S(1)} %dynamic-slice_convert_fusion.4), channel_id=1, source_target_pairs={{0,2},{1,3},{2,0},{3,1},{4,6},{5,7},{6,4},{7,5},{8,10},{9,11},{10,... | collective-permute-start | bytes 1382408 | tf_op jit(solution)/shard_map/ppermute | solution.py:92
  404.3 11.8 %copy-start.14 = (f32[75,24,128]{2,1,0:T(8,128)S(1)}, f32[75,24,128]{2,1,0:T(8,128)}, u32[]{:S(2)}) copy-start(f32[75,24,128]{2,1,0:T(8,128)} %copy-done.13) | copy-start | bytes 2764804
  418.8 11.8 %collective-permute-start.8 = (bf16[1,1800,128]{2,1,0:T(8,128)(2,1)S(1)}, bf16[1,1800,128]{2,1,0:T(8,128)(2,1)S(1)}, u32[]{:S(2)}, u32[]{:S(2)}) collective-permute-start(bf16[1,1800,128]{2,1,0:T(8,128)(2,1)S(1)} %bitcast.188), channel_id=1, source_target_pairs={{0,2},{1,3},{2,0},{3,1},{4,6},{5,7},{6,4},{7,5},{8,10},{9,11},{10,... | collective-permute-start | bytes 1382408 | tf_op jit(solution)/shard_map/ppermute | solution.py:92
  430.9 2.5 collective-permute-start.9
  435.3 1.0 collective-permute-start.10
  436.2 0.8 copy-start.21
  439.9 2.4 copy-start.9
  556.1 2.1 copy-start.4
  591.8 2.5 collective-permute-start.11
  592.2 2.8 copy-start.24
  592.2 3.8 copy-start.15
  594.6 12.6 %collective-permute-start.12 = (bf16[1,1800,128]{2,1,0:T(8,128)(2,1)S(1)}, bf16[1,1800,128]{2,1,0:T(8,128)(2,1)S(1)}, u32[]{:S(2)}, u32[]{:S(2)}) collective-permute-start(bf16[1,1800,128]{2,1,0:T(8,128)(2,1)S(1)} %dynamic-slice_convert_fusion.3), channel_id=1, source_target_pairs={{0,2},{1,3},{2,0},{3,1},{4,6},{5,7},{6,4},{7,5},{8,10},{9,11},{10,... | collective-permute-start | bytes 1382408 | tf_op jit(solution)/shard_map/ppermute | solution.py:92
  595.9 11.4 %copy-start.7 = (f32[300,24,128]{2,1,0:T(8,128)S(1)}, f32[300,24,128]{2,1,0:T(8,128)}, u32[]{:S(2)}) copy-start(f32[300,24,128]{2,1,0:T(8,128)} %copy-done.5) | copy-start | bytes 11059204
  607.7 11.8 %collective-permute-start.13 = (bf16[1,1800,128]{2,1,0:T(8,128)(2,1)S(1)}, bf16[1,1800,128]{2,1,0:T(8,128)(2,1)S(1)}, u32[]{:S(2)}, u32[]{:S(2)}) collective-permute-start(bf16[1,1800,128]{2,1,0:T(8,128)(2,1)S(1)} %bitcast.203), channel_id=1, source_target_pairs={{0,2},{1,3},{2,0},{3,1},{4,6},{5,7},{6,4},{7,5},{8,10},{9,11},{10,... | collective-permute-start | bytes 1382408 | tf_op jit(solution)/shard_map/ppermute | solution.py:92
  619.7 2.5 collective-permute-start.14
Sparse Core Ops, SparseCore 0:
  62.2 101.9 all-gather.3
  245.4 119.2 all-gather.5
  437.2 118.8 all-gather.7
